TPU v7x, 32 devices: a whole 2x2x4 slice. The times are simulated.
32 devices in a mesh: row: 16 (over z, y, core), col: 2 (over x).
Axes of the slice: x: 2, y: 2, z: 4, core: 2. Of those that a mesh axis runs over, the one named last changes fastest.
Arguments:
- stiffness: bfloat16 [32, 768, 768], P(('row', 'col'))
- local_inverse: bfloat16 [32, 768, 768], P(('row', 'col'))
- averaging_basis: bfloat16 [32, 768, 64], P(('row', 'col')), may hold values from -0.4375 to 0.4375
- loads: bfloat16 [32, 768, 128], P(('row', 'col')), may hold values from -6 to 6
- start: float32 [6144, 128], P(('row', 'col')), may hold values from -6 to 6
- coarse_inverse: float32 [16, 2, 24, 768], P(None, 'col', None, 'row')
- sizes: int32 [32], P(('row', 'col')), may hold values from 384 to 768, as said below
- dof_ids: int32 [32, 768], P(('row', 'col')), may hold values from 0 to 6143, as said below
- coarse_ids: int32 [32, 64], P(('row', 'col')), may hold values from 0 to 767, as said below
Outputs:
- solution_field: float32 [6144, 128], P(('row', 'col'))
- residual: float32 [6144, 128], P(('row', 'col'))
Inputs may be any that keep to these rules, and one draw needn't show every extreme that they name: `sizes`: the largest interface order, 768, occurs in every draw. `dof_ids`: subdomain s sits at row s // 2 and column s % 2; global interface dof g is owned by subdomain g // 192. The 768 slots of a subdomain hold distinct dofs, each owned by the subdomain itself or a subdomain at most one row and one column away; slots from sizes[s] on are not used. `coarse_ids`: coarse dof k is owned by subdomain k // 24. The 64 coarse dofs of a subdomain are distinct, each owned by the subdomain itself or a subdomain at most one row and one column away.
All inputs are finite; a program needn't handle non-finite values.
Results may differ from a plain program's by a relative error of at most 0.0064.
Values may be sent and summed in bfloat16 or wider, within the bound.
A program may use at most 64 MiB of HBM per device.

v0:
```python
import jax
import jax.numpy as jnp
from jax import lax
from jax.sharding import PartitionSpec as P

ITERS = 2


HIGHEST_PRECISION = lax.Precision.HIGHEST


def extended(cells, sides, width):
    for axis, dim in sides:
        count = lax.axis_size(axis)
        ends = count - 1
        head = lax.slice_in_dim(cells, 0, width, axis=dim)
        tail = lax.slice_in_dim(cells, cells.shape[dim] - width, cells.shape[dim], axis=dim)
        cells = jnp.concatenate(
            [
                lax.ppermute(tail, axis, [(i, (i + 1) % count) for i in range(ends)]),
                cells,
                lax.ppermute(head, axis, [((i + 1) % count, i) for i in range(ends)]),
            ],
            axis=dim,
        )
    return cells


def window_positions(wanted, per_owner):
    members = lax.axis_size("col")
    owner = wanted // per_owner
    row_step = owner // members - lax.axis_index("row") + 1
    col_step = owner % members - lax.axis_index("col") + 1
    return (row_step * 3 + col_step) * per_owner + wanted % per_owner


def row_positions(wanted, per_row):
    row_step = wanted // per_row - lax.axis_index("row") + 1
    return row_step * per_row + wanted % per_row


def take_rows(window_rows, positions, active):
    picked = jnp.take(window_rows, positions, axis=0, mode="clip")
    keep = active.reshape(active.shape + (1,) * (picked.ndim - 1))
    return jnp.where(keep, picked, jnp.zeros_like(picked))


def to_owners(blocks):
    across = extended(blocks[:, ::2], (("col", 1),), 1)
    middle = blocks[:, 1] + across[:, 0] + across[:, 3]
    downward = extended(middle[::2], (("row", 0),), 1)
    return middle[1] + downward[0] + downward[3]


def owned_window(owned):
    wide = extended(owned[None, None], (("row", 0), ("col", 1)), 1)
    return wide.reshape((-1,) + owned.shape[1:])


def spread_back(positions, active, values, per_owner):
    window_size = 9 * per_owner
    target = jnp.where(active, positions, window_size)
    summed = jax.ops.segment_sum(values, target, num_segments=window_size + 1)[:window_size]
    return to_owners(summed.reshape((3, 3, per_owner) + values.shape[1:]))


def body(
    stiffness,
    local_inverse,
    averaging_basis,
    loads,
    start,
    coarse_inverse,
    sizes,
    dof_ids,
    coarse_ids,
):
    per_owner = start.shape[0]
    per_coarse = coarse_inverse.shape[2]
    order_local = dof_ids.shape[1]
    active = jnp.arange(order_local, dtype=jnp.int32) < sizes[0]
    active_float = active.astype(jnp.float32)
    positions = window_positions(dof_ids[0], per_owner)
    every_primal = jnp.ones((coarse_ids.shape[1],), dtype=bool)
    coarse_positions = window_positions(coarse_ids[0], per_coarse)
    out_positions = row_positions(coarse_ids[0], per_coarse * lax.axis_size("col"))
    count_owned = spread_back(positions, active, active_float, per_owner)
    count_local = jnp.take(owned_window(count_owned), positions, axis=0, mode="clip")
    weight = active_float / (count_local + 1.0 - active_float)
    panel = coarse_inverse.reshape(-1, coarse_inverse.shape[3])
    solution_field = start
    residual = start
    for repeat in range(ITERS):
        iterate_half = solution_field.astype(jnp.bfloat16)
        nearby = extended(iterate_half[None, None], (("row", 0), ("col", 1)), 1)
        local_iterate = take_rows(nearby.reshape(-1, nearby.shape[3]), positions, active)
        image = jnp.dot(stiffness[0], local_iterate, preferred_element_type=jnp.float32)
        residual = spread_back(positions, active, loads[0].astype(jnp.float32) - image, per_owner)
        scaled = (weight[:, None] * take_rows(owned_window(residual), positions, active)).astype(
            jnp.bfloat16
        )
        local_part = jnp.dot(local_inverse[0], scaled, preferred_element_type=jnp.float32)
        primal = lax.dot_general(
            averaging_basis[0], scaled, (((0,), (0,)), ((), ())), preferred_element_type=jnp.float32
        )
        coarse_owned = spread_back(coarse_positions, every_primal, primal, per_coarse)
        coarse_part = lax.dot_general(
            panel,
            lax.all_gather(coarse_owned, "row", axis=0, tiled=True),
            (((0,), (0,)), ((), ())),
            precision=HIGHEST_PRECISION,
            preferred_element_type=jnp.float32,
        )
        totals = lax.psum(coarse_part, "col").astype(jnp.bfloat16)
        beside_all = extended(totals[None], (("row", 0),), 1)
        coarse_local = take_rows(
            beside_all.reshape(-1, beside_all.shape[-1]), out_positions, every_primal
        )
        correction = jnp.dot(averaging_basis[0], coarse_local, preferred_element_type=jnp.float32)
        update = weight[:, None] * (local_part + correction)
        solution_field = solution_field + spread_back(positions, active, update, per_owner)
    return (solution_field, residual)


def solution(mesh):
    in_specs = (
        P(("row", "col"), None, None),
        P(("row", "col"), None, None),
        P(("row", "col"), None, None),
        P(("row", "col"), None, None),
        P(("row", "col"), None),
        P(None, "col", None, "row"),
        P(("row", "col")),
        P(("row", "col"), None),
        P(("row", "col"), None),
    )
    out_specs = (P(("row", "col"), None), P(("row", "col"), None))
    return jax.shard_map(body, mesh=mesh, in_specs=in_specs, out_specs=out_specs, check_vma=False)
```

profile of v0, /device:TPU:0, one launch (start us, length us, event | category | flops | bytes accessed | tf_op | source)
XLA Modules:
  0.0 330.3 jit_solution(6756174343568602535)
XLA Ops:
  2.9 3.0 collective-permute-start.8
  7.4 4.7 %scatter_custom_fusion = f32[1729]{0:T(1024)S(1)} fusion(s32[768]{0:T(1024)S(1)} %get-tuple-element.3, f32[768]{0:T(1024)S(1)} %get-tuple-element.39, f32[]{:T(128)} %constant.96.clone.1), kind=kCustom, calls=%fused_computation.123 | custom fusion | flops 768 | bytes 6920 | tf_op jit(solution)/shard_map/scatter-add | solution.py:63
  12.8 4.9 %collective-permute-start = (f32[3,1,192]{2,1,0:T(1,128)}, f32[3,1,192]{2,1,0:T(1,128)S(1)}, u32[]{:S(2)}, u32[]{:S(2)}) collective-permute-start(f32[3,1,192]{2,1,0:T(1,128)} %get-tuple-element.32), channel_id=1, source_target_pairs={{0,1},{2,3},{4,5},{6,7},{8,9},{10,11},{12,13},{14,15},{16,17},{18,... | collective-permute-start | bytes 6920 | tf_op jit(solution)/shard_map/ppermute | solution.py:20
  17.7 1.3 collective-permute-start.1
  19.1 1.3 collective-permute-start.11
  20.4 5.1 %collective-permute-start.10 = (bf16[3,1,192,128]{3,2,1,0:T(8,128)(2,1)S(1)}, bf16[3,1,192,128]{3,2,1,0:T(8,128)(2,1)S(1)}, u32[]{:S(2)}, u32[]{:S(2)}) collective-permute-start(bf16[3,1,192,128]{3,2,1,0:T(8,128)(2,1)S(1)} %pad_maximum_fusion.6), channel_id=1, source_target_pairs={{0,1},{2,3},{4,5},{6,7},{8,9},{10,11},{12,13},{14,15},{16,17},{18,... | collective-permute-start | bytes 442376 | tf_op jit(solution)/shard_map/ppermute | solution.py:20
  28.2 1.3 collective-permute-done.10
  29.5 1.9 gather_fusion.1
  32.2 6.2 %scatter_custom_fusion.1 = f32[1729,128]{1,0:T(8,128)S(1)} fusion(s32[768]{0:T(1024)S(1)} %get-tuple-element.3, f32[768,128]{1,0:T(8,128)S(1)} %copy.15, f32[]{:T(128)} %constant.96.clone.1), kind=kCustom, calls=%fused_computation.42 | custom fusion | flops 98304 | bytes 885252 | tf_op jit(solution)/shard_map/scatter-add | solution.py:63
  38.6 4.5 %collective-permute-start.12 = (f32[3,1,192,128]{3,2,1,0:T(8,128)S(1)}, f32[3,1,192,128]{3,2,1,0:T(8,128)S(1)}, u32[]{:S(2)}, u32[]{:S(2)}) collective-permute-start(f32[3,1,192,128]{3,2,1,0:T(8,128)S(1)} %get-tuple-element.12), channel_id=1, source_target_pairs={{0,1},{2,3},{4,5},{6,7},{8,9},{10,11},{12,13},{14,15},{16,17},{18,... | collective-permute-start | bytes 884744 | tf_op jit(solution)/shard_map/ppermute | solution.py:20
  43.1 1.3 collective-permute-start.13
  45.2 1.6 collective-permute-start.2
  48.1 1.4 collective-permute-done.12
  49.5 4.1 %collective-permute-done.13 = f32[3,1,192,128]{3,2,1,0:T(8,128)S(1)} collective-permute-done((f32[3,1,192,128]{3,2,1,0:T(8,128)S(1)}, f32[3,1,192,128]{3,2,1,0:T(8,128)S(1)}, u32[]{:S(2)}, u32[]{:S(2)}) %collective-permute-start.13) | collective-permute-done | bytes 294944 | tf_op jit(solution)/shard_map/ppermute | solution.py:22
  53.7 1.3 collective-permute-start.14
  57.7 6.1 %collective-permute-start.4 = (f32[1,1,192]{2,1,0:T(1,128)S(1)}, f32[1,1,192]{2,1,0:T(1,128)S(1)}, u32[]{:S(2)}, u32[]{:S(2)}) collective-permute-start(f32[1,1,192]{2,1,0:T(1,128)S(1)} %fusion.72), channel_id=1, source_target_pairs={{0,2},{2,4},{4,6},{6,8},{8,10},{10,12},{12,14},{14,16},{16,18},{18... | collective-permute-start | bytes 2312 | tf_op jit(solution)/shard_map/ppermute | solution.py:20
  65.1 4.3 %collective-permute-start.16 = (f32[1,1,192,128]{3,2,1,0:T(8,128)S(1)}, f32[1,1,192,128]{3,2,1,0:T(8,128)S(1)}, u32[]{:S(2)}, u32[]{:S(2)}) collective-permute-start(f32[1,1,192,128]{3,2,1,0:T(8,128)S(1)} %fusion.42), channel_id=1, source_target_pairs={{0,2},{2,4},{4,6},{6,8},{8,10},{10,12},{12,14},{14,16},{16,18},{18... | collective-permute-start | bytes 294920 | tf_op jit(solution)/shard_map/ppermute | solution.py:20
  70.7 4.5 %collective-permute-start.6 = (f32[3,1,192]{2,1,0:T(1,128)S(1)}, f32[3,1,192]{2,1,0:T(1,128)S(1)}, u32[]{:S(2)}, u32[]{:S(2)}) collective-permute-start(f32[3,1,192]{2,1,0:T(1,128)S(1)} %pad_maximum_fusion.11), channel_id=1, source_target_pairs={{0,1},{2,3},{4,5},{6,7},{8,9},{10,11},{12,13},{14,15},{16,17},{18,... | collective-permute-start | bytes 6920 | tf_op jit(solution)/shard_map/ppermute | solution.py:20
  76.6 4.6 %collective-permute-start.18 = (f32[3,1,192,128]{3,2,1,0:T(8,128)S(1)}, f32[3,1,192,128]{3,2,1,0:T(8,128)S(1)}, u32[]{:S(2)}, u32[]{:S(2)}) collective-permute-start(f32[3,1,192,128]{3,2,1,0:T(8,128)S(1)} %pad_maximum_fusion.4), channel_id=1, source_target_pairs={{0,1},{2,3},{4,5},{6,7},{8,9},{10,11},{12,13},{14,15},{16,17},{18,... | collective-permute-start | bytes 884744 | tf_op jit(solution)/shard_map/ppermute | solution.py:20
  81.3 4.5 %gather_fusion = f32[768]{0:T(1024)S(1)} fusion(f32[1728]{0:T(1024)S(1)} %reshape.566, s32[1024]{0:T(1024)S(1)} %pad_clamp_fusion.1), kind=kCustom, calls=%fused_computation | custom fusion | bytes 9216 | tf_op jit(solution)/shard_map/jit(_take)/gather | solution.py:88
  86.9 1.6 collective-permute-done.18
  88.6 1.6 gather_fusion.2
  91.7 4.4 %collective-permute-start.20 = (f32[3,1,24,128]{3,2,1,0:T(8,128)S(1)}, f32[3,1,24,128]{3,2,1,0:T(8,128)S(1)}, u32[]{:S(2)}, u32[]{:S(2)}) collective-permute-start(f32[3,1,24,128]{3,2,1,0:T(8,128)S(1)} %get-tuple-element.26), channel_id=1, source_target_pairs={{0,1},{2,3},{4,5},{6,7},{8,9},{10,11},{12,13},{14,15},{16,17},{18,... | collective-permute-start | bytes 110600 | tf_op jit(solution)/shard_map/ppermute | solution.py:20
  97.7 4.2 %collective-permute-done.21 = f32[3,1,24,128]{3,2,1,0:T(8,128)S(1)} collective-permute-done((f32[3,1,24,128]{3,2,1,0:T(8,128)S(1)}, f32[3,1,24,128]{3,2,1,0:T(8,128)S(1)}, u32[]{:S(2)}, u32[]{:S(2)}) %collective-permute-start.21) | collective-permute-done | bytes 36896 | tf_op jit(solution)/shard_map/ppermute | solution.py:22
  104.7 3.0 collective-permute-done.23
  107.6 20.6 %all-gather = f32[1,384,128]{2,1,0:T(8,128)S(1)} all-gather(f32[1,24,128]{2,1,0:T(8,128)S(1)} %fusion.58), channel_id=2, replica_groups=mesh['row'=16,'col'=2] {'row'}, dimensions={1}, use_global_device_ids=true | all-gather | bytes 208896 | tf_op jit(solution)/shard_map/all_gather | solution.py:109
  128.8 6.8 %psum.14 = bf16[48,128]{1,0:T(8,128)(2,1)S(1)} all-reduce(f32[48,128]{1,0:T(8,128)S(1)} %convolution_bitcast_fusion.5), channel_id=1, replica_groups=mesh['row'=16,'col'=2] {'col'}, use_global_device_ids=true, to_apply=%region_3.4 | all-reduce | flops 6144 | bytes 36864 | tf_op jit(solution)/shard_map/psum | solution.py:114
  136.9 3.2 collective-permute-start.24
  142.8 6.6 %scatter_custom_fusion.3 = f32[1729,128]{1,0:T(8,128)S(1)} fusion(s32[768]{0:T(1024)} %copy-done.10, f32[768,128]{1,0:T(8,128)} %copy.16, f32[]{:T(128)} %constant.96.clone.1), kind=kCustom, calls=%fused_computation.40 | custom fusion | flops 98304 | bytes 885760 | tf_op jit(solution)/shard_map/scatter-add | solution.py:63
  149.6 4.1 %collective-permute-start.26 = (f32[3,1,192,128]{3,2,1,0:T(8,128)S(1)}, f32[3,1,192,128]{3,2,1,0:T(8,128)S(1)}, u32[]{:S(2)}, u32[]{:S(2)}) collective-permute-start(f32[3,1,192,128]{3,2,1,0:T(8,128)S(1)} %get-tuple-element.10), channel_id=1, source_target_pairs={{0,1},{2,3},{4,5},{6,7},{8,9},{10,11},{12,13},{14,15},{16,17},{18,... | collective-permute-start | bytes 884744 | tf_op jit(solution)/shard_map/ppermute | solution.py:20
  155.0 6.0 %collective-permute-done.26 = f32[3,1,192,128]{3,2,1,0:T(8,128)S(1)} collective-permute-done((f32[3,1,192,128]{3,2,1,0:T(8,128)S(1)}, f32[3,1,192,128]{3,2,1,0:T(8,128)S(1)}, u32[]{:S(2)}, u32[]{:S(2)}) %collective-permute-start.26) | collective-permute-done | bytes 294944 | tf_op jit(solution)/shard_map/ppermute | solution.py:20
  161.0 4.1 %collective-permute-done.27 = f32[3,1,192,128]{3,2,1,0:T(8,128)S(1)} collective-permute-done((f32[3,1,192,128]{3,2,1,0:T(8,128)S(1)}, f32[3,1,192,128]{3,2,1,0:T(8,128)S(1)}, u32[]{:S(2)}, u32[]{:S(2)}) %collective-permute-start.27) | collective-permute-done | bytes 294944 | tf_op jit(solution)/shard_map/ppermute | solution.py:22
  165.2 1.7 collective-permute-start.28
  168.2 2.9 collective-permute-done.29
  173.0 5.8 %collective-permute-start.30 = (bf16[1,1,192,128]{3,2,1,0:T(8,128)(2,1)S(1)}, bf16[1,1,192,128]{3,2,1,0:T(8,128)(2,1)S(1)}, u32[]{:S(2)}, u32[]{:S(2)}) collective-permute-start(bf16[1,1,192,128]{3,2,1,0:T(8,128)(2,1)S(1)} %get-tuple-element.4), channel_id=1, source_target_pairs={{0,2},{2,4},{4,6},{6,8},{8,10},{10,12},{12,14},{14,16},{16,18},{18... | collective-permute-start | bytes 147464 | tf_op jit(solution)/shard_map/ppermute | solution.py:20
  181.0 4.6 %collective-permute-start.32 = (bf16[3,1,192,128]{3,2,1,0:T(8,128)(2,1)S(1)}, bf16[3,1,192,128]{3,2,1,0:T(8,128)(2,1)S(1)}, u32[]{:S(2)}, u32[]{:S(2)}) collective-permute-start(bf16[3,1,192,128]{3,2,1,0:T(8,128)(2,1)S(1)} %pad_maximum_fusion.7), channel_id=1, source_target_pairs={{0,1},{2,3},{4,5},{6,7},{8,9},{10,11},{12,13},{14,15},{16,17},{18,... | collective-permute-start | bytes 442376 | tf_op jit(solution)/shard_map/ppermute | solution.py:20
  185.5 1.7 collective-permute-done.33
  187.2 1.7 collective-permute-done.32
  189.0 1.9 gather_fusion.4
  192.5 6.6 %scatter_custom_fusion.4 = f32[1729,128]{1,0:T(8,128)S(1)} fusion(s32[768]{0:T(1024)} %copy-done.10, f32[768,128]{1,0:T(8,128)} %copy.17, f32[]{:T(128)} %constant.96.clone.1), kind=kCustom, calls=%fused_computation.38 | custom fusion | flops 98304 | bytes 885760 | tf_op jit(solution)/shard_map/scatter-add | solution.py:63
  199.2 4.5 %collective-permute-start.34 = (f32[3,1,192,128]{3,2,1,0:T(8,128)S(1)}, f32[3,1,192,128]{3,2,1,0:T(8,128)S(1)}, u32[]{:S(2)}, u32[]{:S(2)}) collective-permute-start(f32[3,1,192,128]{3,2,1,0:T(8,128)S(1)} %get-tuple-element.8), channel_id=1, source_target_pairs={{0,1},{2,3},{4,5},{6,7},{8,9},{10,11},{12,13},{14,15},{16,17},{18,... | collective-permute-start | bytes 884744 | tf_op jit(solution)/shard_map/ppermute | solution.py:20
  205.0 5.8 %collective-permute-done.34 = f32[3,1,192,128]{3,2,1,0:T(8,128)S(1)} collective-permute-done((f32[3,1,192,128]{3,2,1,0:T(8,128)S(1)}, f32[3,1,192,128]{3,2,1,0:T(8,128)S(1)}, u32[]{:S(2)}, u32[]{:S(2)}) %collective-permute-start.34) | collective-permute-done | bytes 294944 | tf_op jit(solution)/shard_map/ppermute | solution.py:20
  210.9 4.1 %collective-permute-done.35 = f32[3,1,192,128]{3,2,1,0:T(8,128)S(1)} collective-permute-done((f32[3,1,192,128]{3,2,1,0:T(8,128)S(1)}, f32[3,1,192,128]{3,2,1,0:T(8,128)S(1)}, u32[]{:S(2)}, u32[]{:S(2)}) %collective-permute-start.35) | collective-permute-done | bytes 294944 | tf_op jit(solution)/shard_map/ppermute | solution.py:22
  215.1 1.5 collective-permute-start.36
  217.9 5.2 %collective-permute-done.37 = f32[1,192,128]{2,1,0:T(8,128)S(1)} collective-permute-done((f32[1,192,128]{2,1,0:T(8,128)S(1)}, f32[1,192,128]{2,1,0:T(8,128)S(1)}, u32[]{:S(2)}, u32[]{:S(2)}) %collective-permute-start.37) | collective-permute-done | bytes 98336 | tf_op jit(solution)/shard_map/ppermute | solution.py:22
  225.0 5.8 %collective-permute-start.38 = (f32[1,1,192,128]{3,2,1,0:T(8,128)S(1)}, f32[1,1,192,128]{3,2,1,0:T(8,128)S(1)}, u32[]{:S(2)}, u32[]{:S(2)}) collective-permute-start(f32[1,1,192,128]{3,2,1,0:T(8,128)S(1)} %get-tuple-element.15), channel_id=1, source_target_pairs={{0,2},{2,4},{4,6},{6,8},{8,10},{10,12},{12,14},{14,16},{16,18},{18... | collective-permute-start | bytes 294920 | tf_op jit(solution)/shard_map/ppermute | solution.py:20
  233.1 4.6 %collective-permute-start.40 = (f32[3,1,192,128]{3,2,1,0:T(8,128)S(1)}, f32[3,1,192,128]{3,2,1,0:T(8,128)S(1)}, u32[]{:S(2)}, u32[]{:S(2)}) collective-permute-start(f32[3,1,192,128]{3,2,1,0:T(8,128)S(1)} %pad_maximum_fusion.5), channel_id=1, source_target_pairs={{0,1},{2,3},{4,5},{6,7},{8,9},{10,11},{12,13},{14,15},{16,17},{18,... | collective-permute-start | bytes 884744 | tf_op jit(solution)/shard_map/ppermute | solution.py:20
  237.6 3.5 %collective-permute-done.41 = f32[3,1,192,128]{3,2,1,0:T(8,128)S(1)} collective-permute-done((f32[3,1,192,128]{3,2,1,0:T(8,128)S(1)}, f32[3,1,192,128]{3,2,1,0:T(8,128)S(1)}, u32[]{:S(2)}, u32[]{:S(2)}) %collective-permute-start.41) | collective-permute-done | bytes 294944 | tf_op jit(solution)/shard_map/ppermute | solution.py:22
  241.2 1.8 collective-permute-done.40
  243.0 2.3 gather_fusion.5
  245.3 1.5 convolution_bitcast_fusion.2
  247.7 4.4 %collective-permute-start.42 = (f32[3,1,24,128]{3,2,1,0:T(8,128)S(1)}, f32[3,1,24,128]{3,2,1,0:T(8,128)S(1)}, u32[]{:S(2)}, u32[]{:S(2)}) collective-permute-start(f32[3,1,24,128]{3,2,1,0:T(8,128)S(1)} %get-tuple-element.24), channel_id=1, source_target_pairs={{0,1},{2,3},{4,5},{6,7},{8,9},{10,11},{12,13},{14,15},{16,17},{18,... | collective-permute-start | bytes 110600 | tf_op jit(solution)/shard_map/ppermute | solution.py:20
  253.7 4.2 %collective-permute-done.43 = f32[3,1,24,128]{3,2,1,0:T(8,128)S(1)} collective-permute-done((f32[3,1,24,128]{3,2,1,0:T(8,128)S(1)}, f32[3,1,24,128]{3,2,1,0:T(8,128)S(1)}, u32[]{:S(2)}, u32[]{:S(2)}) %collective-permute-start.43) | collective-permute-done | bytes 36896 | tf_op jit(solution)/shard_map/ppermute | solution.py:22
  258.0 2.4 collective-permute-start.44
  261.7 7.5 %collective-permute-done.45 = f32[1,24,128]{2,1,0:T(8,128)S(1)} collective-permute-done((f32[1,24,128]{2,1,0:T(8,128)S(1)}, f32[1,24,128]{2,1,0:T(8,128)S(1)}, u32[]{:S(2)}, u32[]{:S(2)}) %collective-permute-start.45) | collective-permute-done | bytes 12320 | tf_op jit(solution)/shard_map/ppermute | solution.py:22
  269.2 20.0 %all-gather.1 = f32[1,384,128]{2,1,0:T(8,128)S(1)} all-gather(f32[1,24,128]{2,1,0:T(8,128)S(1)} %fusion.56), channel_id=3, replica_groups=mesh['row'=16,'col'=2] {'row'}, dimensions={1}, use_global_device_ids=true | all-gather | bytes 208896 | tf_op jit(solution)/shard_map/all_gather | solution.py:109
  289.7 6.8 %psum.15 = bf16[48,128]{1,0:T(8,128)(2,1)S(1)} all-reduce(f32[48,128]{1,0:T(8,128)S(1)} %convolution_bitcast_fusion.4), channel_id=1, replica_groups=mesh['row'=16,'col'=2] {'col'}, use_global_device_ids=true, to_apply=%region_7.8 | all-reduce | flops 6144 | bytes 36864 | tf_op jit(solution)/shard_map/psum | solution.py:114
  297.8 3.3 collective-permute-start.46
  303.1 6.3 %scatter_custom_fusion.6 = f32[1729,128]{1,0:T(8,128)S(1)} fusion(s32[768]{0:T(1024)} %copy-done.10, f32[768,128]{1,0:T(8,128)S(1)} %copy.18, f32[]{:T(128)} %constant.96.clone.1), kind=kCustom, calls=%fused_computation.36 | custom fusion | flops 98304 | bytes 885760 | tf_op jit(solution)/shard_map/scatter-add | solution.py:63
  309.6 4.1 %collective-permute-start.48 = (f32[3,1,192,128]{3,2,1,0:T(8,128)S(1)}, f32[3,1,192,128]{3,2,1,0:T(8,128)S(1)}, u32[]{:S(2)}, u32[]{:S(2)}) collective-permute-start(f32[3,1,192,128]{3,2,1,0:T(8,128)S(1)} %get-tuple-element.6), channel_id=1, source_target_pairs={{0,1},{2,3},{4,5},{6,7},{8,9},{10,11},{12,13},{14,15},{16,17},{18,... | collective-permute-start | bytes 884744 | tf_op jit(solution)/shard_map/ppermute | solution.py:20
  315.1 5.3 %collective-permute-done.48 = f32[3,1,192,128]{3,2,1,0:T(8,128)S(1)} collective-permute-done((f32[3,1,192,128]{3,2,1,0:T(8,128)S(1)}, f32[3,1,192,128]{3,2,1,0:T(8,128)S(1)}, u32[]{:S(2)}, u32[]{:S(2)}) %collective-permute-start.48) | collective-permute-done | bytes 294944 | tf_op jit(solution)/shard_map/ppermute | solution.py:20
  320.4 4.1 %collective-permute-done.49 = f32[3,1,192,128]{3,2,1,0:T(8,128)S(1)} collective-permute-done((f32[3,1,192,128]{3,2,1,0:T(8,128)S(1)}, f32[3,1,192,128]{3,2,1,0:T(8,128)S(1)}, u32[]{:S(2)}, u32[]{:S(2)}) %collective-permute-start.49) | collective-permute-done | bytes 294944 | tf_op jit(solution)/shard_map/ppermute | solution.py:22
  324.6 1.3 collective-permute-start.50
  327.2 2.4 collective-permute-done.51
  (167 shorter events, 54.1 us)
Async XLA Ops:
  0.6 30.8 %copy-start = (bf16[1,768,768]{2,1,0:T(8,128)(2,1)S(1)}, bf16[1,768,768]{2,1,0:T(8,128)(2,1)}, u32[]{:S(2)}) copy-start(bf16[1,768,768]{2,1,0:T(8,128)(2,1)} %param.9) | copy-start | bytes 3538948
  1.6 17.4 %collective-permute-start.9 = (bf16[1,1,192,128]{3,2,1,0:T(8,128)(2,1)S(1)}, bf16[1,1,192,128]{3,2,1,0:T(8,128)(2,1)S(1)}, u32[]{:S(2)}, u32[]{:S(2)}) collective-permute-start(bf16[1,1,192,128]{3,2,1,0:T(8,128)(2,1)S(1)} %convert_bitcast_fusion.1), channel_id=1, source_target_pairs={{2,0},{4,2},{6,4},{8,6},{10,8},{12,10},{14,12},{16,14},{18,16},{20... | collective-permute-start | bytes 147464 | tf_op jit(solution)/shard_map/ppermute | solution.py:22
  2.9 16.1 %collective-permute-start.8 = (bf16[1,1,192,128]{3,2,1,0:T(8,128)(2,1)S(1)}, bf16[1,1,192,128]{3,2,1,0:T(8,128)(2,1)S(1)}, u32[]{:S(2)}, u32[]{:S(2)}) collective-permute-start(bf16[1,1,192,128]{3,2,1,0:T(8,128)(2,1)S(1)} %convert_bitcast_fusion.1), channel_id=1, source_target_pairs={{0,2},{2,4},{4,6},{6,8},{8,10},{10,12},{12,14},{14,16},{16,18},{18... | collective-permute-start | bytes 147464 | tf_op jit(solution)/shard_map/ppermute | solution.py:20
  7.4 24.8 %copy-start.10 = (s32[768]{0:T(1024)}, s32[768]{0:T(1024)S(1)}, u32[]{:S(2)}) copy-start(s32[768]{0:T(1024)S(1)} %get-tuple-element.3) | copy-start | bytes 9220
  12.2 13.3 %copy-start.8 = (f32[3,3,192]{2,1,0:T(4,128)}, f32[3,3,192]{2,1,0:T(4,128)S(1)}, u32[]{:S(2)}) copy-start(f32[3,3,192]{2,1,0:T(4,128)S(1)} %reshape.565) | copy-start | bytes 20740
  12.8 31.6 %collective-permute-start = (f32[3,1,192]{2,1,0:T(1,128)}, f32[3,1,192]{2,1,0:T(1,128)S(1)}, u32[]{:S(2)}, u32[]{:S(2)}) collective-permute-start(f32[3,1,192]{2,1,0:T(1,128)} %get-tuple-element.32), channel_id=1, source_target_pairs={{0,1},{2,3},{4,5},{6,7},{8,9},{10,11},{12,13},{14,15},{16,17},{18,... | collective-permute-start | bytes 6920 | tf_op jit(solution)/shard_map/ppermute | solution.py:20
  17.7 26.7 %collective-permute-start.1 = (f32[3,1,192]{2,1,0:T(1,128)S(1)}, f32[3,1,192]{2,1,0:T(1,128)}, u32[]{:S(2)}, u32[]{:S(2)}) collective-permute-start(f32[3,1,192]{2,1,0:T(1,128)S(1)} %get-tuple-element.33), channel_id=1, source_target_pairs={{1,0},{3,2},{5,4},{7,6},{9,8},{11,10},{13,12},{15,14},{17,16},{19,... | collective-permute-start | bytes 6920 | tf_op jit(solution)/shard_map/ppermute | solution.py:22
  19.1 9.1 %collective-permute-start.11 = (bf16[3,1,192,128]{3,2,1,0:T(8,128)(2,1)S(1)}, bf16[3,1,192,128]{3,2,1,0:T(8,128)(2,1)S(1)}, u32[]{:S(2)}, u32[]{:S(2)}) collective-permute-start(bf16[3,1,192,128]{3,2,1,0:T(8,128)(2,1)S(1)} %pad_maximum_fusion.6), channel_id=1, source_target_pairs={{1,0},{3,2},{5,4},{7,6},{9,8},{11,10},{13,12},{15,14},{17,16},{19,... | collective-permute-start | bytes 442376 | tf_op jit(solution)/shard_map/ppermute | solution.py:22
  20.4 9.1 %collective-permute-start.10 = (bf16[3,1,192,128]{3,2,1,0:T(8,128)(2,1)S(1)}, bf16[3,1,192,128]{3,2,1,0:T(8,128)(2,1)S(1)}, u32[]{:S(2)}, u32[]{:S(2)}) collective-permute-start(bf16[3,1,192,128]{3,2,1,0:T(8,128)(2,1)S(1)} %pad_maximum_fusion.6), channel_id=1, source_target_pairs={{0,1},{2,3},{4,5},{6,7},{8,9},{10,11},{12,13},{14,15},{16,17},{18,... | collective-permute-start | bytes 442376 | tf_op jit(solution)/shard_map/ppermute | solution.py:20
  38.6 10.9 %collective-permute-start.12 = (f32[3,1,192,128]{3,2,1,0:T(8,128)S(1)}, f32[3,1,192,128]{3,2,1,0:T(8,128)S(1)}, u32[]{:S(2)}, u32[]{:S(2)}) collective-permute-start(f32[3,1,192,128]{3,2,1,0:T(8,128)S(1)} %get-tuple-element.12), channel_id=1, source_target_pairs={{0,1},{2,3},{4,5},{6,7},{8,9},{10,11},{12,13},{14,15},{16,17},{18,... | collective-permute-start | bytes 884744 | tf_op jit(solution)/shard_map/ppermute | solution.py:20
  43.1 10.5 %collective-permute-start.13 = (f32[3,1,192,128]{3,2,1,0:T(8,128)S(1)}, f32[3,1,192,128]{3,2,1,0:T(8,128)S(1)}, u32[]{:S(2)}, u32[]{:S(2)}) collective-permute-start(f32[3,1,192,128]{3,2,1,0:T(8,128)S(1)} %get-tuple-element.13), channel_id=1, source_target_pairs={{1,0},{3,2},{5,4},{7,6},{9,8},{11,10},{13,12},{15,14},{17,16},{19,... | collective-permute-start | bytes 884744 | tf_op jit(solution)/shard_map/ppermute | solution.py:22
  45.2 11.1 %collective-permute-start.2 = (f32[1,192]{1,0:T(1,128)S(1)}, f32[1,192]{1,0:T(1,128)S(1)}, u32[]{:S(2)}, u32[]{:S(2)}) collective-permute-start(f32[1,192]{1,0:T(1,128)S(1)} %get-tuple-element.34), channel_id=1, source_target_pairs={{0,2},{2,4},{4,6},{6,8},{8,10},{10,12},{12,14},{14,16},{16,18},{18... | collective-permute-start | bytes 2312 | tf_op jit(solution)/shard_map/ppermute | solution.py:20
  46.8 9.5 %collective-permute-start.3 = (f32[1,192]{1,0:T(1,128)S(1)}, f32[1,192]{1,0:T(1,128)S(1)}, u32[]{:S(2)}, u32[]{:S(2)}) collective-permute-start(f32[1,192]{1,0:T(1,128)S(1)} %get-tuple-element.35), channel_id=1, source_target_pairs={{2,0},{4,2},{6,4},{8,6},{10,8},{12,10},{14,12},{16,14},{18,16},{20... | collective-permute-start | bytes 2312 | tf_op jit(solution)/shard_map/ppermute | solution.py:22
  53.7 10.0 %collective-permute-start.14 = (f32[1,192,128]{2,1,0:T(8,128)S(1)}, f32[1,192,128]{2,1,0:T(8,128)S(1)}, u32[]{:S(2)}, u32[]{:S(2)}) collective-permute-start(f32[1,192,128]{2,1,0:T(8,128)S(1)} %get-tuple-element.22), channel_id=1, source_target_pairs={{0,2},{2,4},{4,6},{6,8},{8,10},{10,12},{12,14},{14,16},{16,18},{18... | collective-permute-start | bytes 294920 | tf_op jit(solution)/shard_map/ppermute | solution.py:20
  55.0 8.7 %collective-permute-start.15 = (f32[1,192,128]{2,1,0:T(8,128)S(1)}, f32[1,192,128]{2,1,0:T(8,128)S(1)}, u32[]{:S(2)}, u32[]{:S(2)}) collective-permute-start(f32[1,192,128]{2,1,0:T(8,128)S(1)} %get-tuple-element.23), channel_id=1, source_target_pairs={{2,0},{4,2},{6,4},{8,6},{10,8},{12,10},{14,12},{16,14},{18,16},{20... | collective-permute-start | bytes 294920 | tf_op jit(solution)/shard_map/ppermute | solution.py:22
  56.4 13.0 %collective-permute-start.5 = (f32[1,1,192]{2,1,0:T(1,128)S(1)}, f32[1,1,192]{2,1,0:T(1,128)S(1)}, u32[]{:S(2)}, u32[]{:S(2)}) collective-permute-start(f32[1,1,192]{2,1,0:T(1,128)S(1)} %fusion.72), channel_id=1, source_target_pairs={{2,0},{4,2},{6,4},{8,6},{10,8},{12,10},{14,12},{16,14},{18,16},{20... | collective-permute-start | bytes 2312 | tf_op jit(solution)/shard_map/ppermute | solution.py:22
  57.7 11.7 %collective-permute-start.4 = (f32[1,1,192]{2,1,0:T(1,128)S(1)}, f32[1,1,192]{2,1,0:T(1,128)S(1)}, u32[]{:S(2)}, u32[]{:S(2)}) collective-permute-start(f32[1,1,192]{2,1,0:T(1,128)S(1)} %fusion.72), channel_id=1, source_target_pairs={{0,2},{2,4},{4,6},{6,8},{8,10},{10,12},{12,14},{14,16},{16,18},{18... | collective-permute-start | bytes 2312 | tf_op jit(solution)/shard_map/ppermute | solution.py:20
  63.8 11.5 %collective-permute-start.17 = (f32[1,1,192,128]{3,2,1,0:T(8,128)S(1)}, f32[1,1,192,128]{3,2,1,0:T(8,128)S(1)}, u32[]{:S(2)}, u32[]{:S(2)}) collective-permute-start(f32[1,1,192,128]{3,2,1,0:T(8,128)S(1)} %fusion.42), channel_id=1, source_target_pairs={{2,0},{4,2},{6,4},{8,6},{10,8},{12,10},{14,12},{16,14},{18,16},{20... | collective-permute-start | bytes 294920 | tf_op jit(solution)/shard_map/ppermute | solution.py:22
  65.1 10.2 %collective-permute-start.16 = (f32[1,1,192,128]{3,2,1,0:T(8,128)S(1)}, f32[1,1,192,128]{3,2,1,0:T(8,128)S(1)}, u32[]{:S(2)}, u32[]{:S(2)}) collective-permute-start(f32[1,1,192,128]{3,2,1,0:T(8,128)S(1)} %fusion.42), channel_id=1, source_target_pairs={{0,2},{2,4},{4,6},{6,8},{8,10},{10,12},{12,14},{14,16},{16,18},{18... | collective-permute-start | bytes 294920 | tf_op jit(solution)/shard_map/ppermute | solution.py:20
  69.4 11.8 %collective-permute-start.7 = (f32[3,1,192]{2,1,0:T(1,128)S(1)}, f32[3,1,192]{2,1,0:T(1,128)S(1)}, u32[]{:S(2)}, u32[]{:S(2)}) collective-permute-start(f32[3,1,192]{2,1,0:T(1,128)S(1)} %pad_maximum_fusion.11), channel_id=1, source_target_pairs={{1,0},{3,2},{5,4},{7,6},{9,8},{11,10},{13,12},{15,14},{17,16},{19,... | collective-permute-start | bytes 6920 | tf_op jit(solution)/shard_map/ppermute | solution.py:22
  70.7 10.5 %collective-permute-start.6 = (f32[3,1,192]{2,1,0:T(1,128)S(1)}, f32[3,1,192]{2,1,0:T(1,128)S(1)}, u32[]{:S(2)}, u32[]{:S(2)}) collective-permute-start(f32[3,1,192]{2,1,0:T(1,128)S(1)} %pad_maximum_fusion.11), channel_id=1, source_target_pairs={{0,1},{2,3},{4,5},{6,7},{8,9},{10,11},{12,13},{14,15},{16,17},{18,... | collective-permute-start | bytes 6920 | tf_op jit(solution)/shard_map/ppermute | solution.py:20
  75.3 11.6 %collective-permute-start.19 = (f32[3,1,192,128]{3,2,1,0:T(8,128)S(1)}, f32[3,1,192,128]{3,2,1,0:T(8,128)S(1)}, u32[]{:S(2)}, u32[]{:S(2)}) collective-permute-start(f32[3,1,192,128]{3,2,1,0:T(8,128)S(1)} %pad_maximum_fusion.4), channel_id=1, source_target_pairs={{1,0},{3,2},{5,4},{7,6},{9,8},{11,10},{13,12},{15,14},{17,16},{19,... | collective-permute-start | bytes 884744 | tf_op jit(solution)/shard_map/ppermute | solution.py:22
  76.6 11.9 %collective-permute-start.18 = (f32[3,1,192,128]{3,2,1,0:T(8,128)S(1)}, f32[3,1,192,128]{3,2,1,0:T(8,128)S(1)}, u32[]{:S(2)}, u32[]{:S(2)}) collective-permute-start(f32[3,1,192,128]{3,2,1,0:T(8,128)S(1)} %pad_maximum_fusion.4), channel_id=1, source_target_pairs={{0,1},{2,3},{4,5},{6,7},{8,9},{10,11},{12,13},{14,15},{16,17},{18,... | collective-permute-start | bytes 884744 | tf_op jit(solution)/shard_map/ppermute | solution.py:20
  88.6 1.6 copy-start.3
  90.2 14.5 %copy-start.11 = (s32[64]{0:T(128)S(1)}, s32[64]{0:T(128)}, u32[]{:S(2)}) copy-start(s32[64]{0:T(128)} %get-tuple-element.36) | copy-start | bytes 772
  90.2 38.1 %copy-start.4 = (f32[16,1,24,48]{3,2,1,0:T(8,128)S(1)}, f32[16,1,24,48]{3,2,1,0:T(8,128)}, u32[]{:S(2)}) copy-start(f32[16,1,24,48]{3,2,1,0:T(8,128)} %param.14) | copy-start | bytes 221188
  90.2 49.9 %copy-start.1 = (bf16[1,768,768]{2,1,0:T(8,128)(2,1)S(1)}, bf16[1,768,768]{2,1,0:T(8,128)(2,1)}, u32[]{:S(2)}) copy-start(bf16[1,768,768]{2,1,0:T(8,128)(2,1)} %param.10) | copy-start | bytes 3538948
  91.7 6.0 %collective-permute-start.20 = (f32[3,1,24,128]{3,2,1,0:T(8,128)S(1)}, f32[3,1,24,128]{3,2,1,0:T(8,128)S(1)}, u32[]{:S(2)}, u32[]{:S(2)}) collective-permute-start(f32[3,1,24,128]{3,2,1,0:T(8,128)S(1)} %get-tuple-element.26), channel_id=1, source_target_pairs={{0,1},{2,3},{4,5},{6,7},{8,9},{10,11},{12,13},{14,15},{16,17},{18,... | collective-permute-start | bytes 110600 | tf_op jit(solution)/shard_map/ppermute | solution.py:20
  96.1 5.9 %collective-permute-start.21 = (f32[3,1,24,128]{3,2,1,0:T(8,128)S(1)}, f32[3,1,24,128]{3,2,1,0:T(8,128)S(1)}, u32[]{:S(2)}, u32[]{:S(2)}) collective-permute-start(f32[3,1,24,128]{3,2,1,0:T(8,128)S(1)} %get-tuple-element.27), channel_id=1, source_target_pairs={{1,0},{3,2},{5,4},{7,6},{9,8},{11,10},{13,12},{15,14},{17,16},{19,... | collective-permute-start | bytes 110600 | tf_op jit(solution)/shard_map/ppermute | solution.py:22
  102.0 2.6 collective-permute-start.22
  103.3 4.3 %collective-permute-start.23 = (f32[1,24,128]{2,1,0:T(8,128)S(1)}, f32[1,24,128]{2,1,0:T(8,128)S(1)}, u32[]{:S(2)}, u32[]{:S(2)}) collective-permute-start(f32[1,24,128]{2,1,0:T(8,128)S(1)} %get-tuple-element.31), channel_id=1, source_target_pairs={{2,0},{4,2},{6,4},{8,6},{10,8},{12,10},{14,12},{16,14},{18,16},{20... | collective-permute-start | bytes 36872 | tf_op jit(solution)/shard_map/ppermute | solution.py:22
  104.6 36.3 %copy-start.9 = (s32[1024]{0:T(1024)}, s32[1024]{0:T(1024)S(1)}, u32[]{:S(2)}) copy-start(s32[1024]{0:T(1024)S(1)} %pad_clamp_fusion) | copy-start | bytes 12292
  135.6 5.3 %collective-permute-start.25 = (bf16[1,48,128]{2,1,0:T(8,128)(2,1)S(1)}, bf16[1,48,128]{2,1,0:T(8,128)(2,1)S(1)}, u32[]{:S(2)}, u32[]{:S(2)}) collective-permute-start(bf16[1,48,128]{2,1,0:T(8,128)(2,1)S(1)} %bitcast.255), channel_id=1, source_target_pairs={{2,0},{4,2},{6,4},{8,6},{10,8},{12,10},{14,12},{16,14},{18,16},{20... | collective-permute-start | bytes 36872 | tf_op jit(solution)/shard_map/ppermute | solution.py:22
  136.9 4.0 %collective-permute-start.24 = (bf16[1,48,128]{2,1,0:T(8,128)(2,1)S(1)}, bf16[1,48,128]{2,1,0:T(8,128)(2,1)S(1)}, u32[]{:S(2)}, u32[]{:S(2)}) collective-permute-start(bf16[1,48,128]{2,1,0:T(8,128)(2,1)S(1)} %bitcast.256), channel_id=1, source_target_pairs={{0,2},{2,4},{4,6},{6,8},{8,10},{10,12},{12,14},{14,16},{16,18},{18... | collective-permute-start | bytes 36872 | tf_op jit(solution)/shard_map/ppermute | solution.py:20
  149.5 21.5 %copy-start.6 = (f32[192,128]{1,0:T(8,128)S(1)}, f32[192,128]{1,0:T(8,128)}, u32[]{:S(2)}) copy-start(f32[192,128]{1,0:T(8,128)} %param.13) | copy-start | bytes 294916
  149.6 11.4 %collective-permute-start.26 = (f32[3,1,192,128]{3,2,1,0:T(8,128)S(1)}, f32[3,1,192,128]{3,2,1,0:T(8,128)S(1)}, u32[]{:S(2)}, u32[]{:S(2)}) collective-permute-start(f32[3,1,192,128]{3,2,1,0:T(8,128)S(1)} %get-tuple-element.10), channel_id=1, source_target_pairs={{0,1},{2,3},{4,5},{6,7},{8,9},{10,11},{12,13},{14,15},{16,17},{18,... | collective-permute-start | bytes 884744 | tf_op jit(solution)/shard_map/ppermute | solution.py:20
  153.7 11.4 %collective-permute-start.27 = (f32[3,1,192,128]{3,2,1,0:T(8,128)S(1)}, f32[3,1,192,128]{3,2,1,0:T(8,128)S(1)}, u32[]{:S(2)}, u32[]{:S(2)}) collective-permute-start(f32[3,1,192,128]{3,2,1,0:T(8,128)S(1)} %get-tuple-element.11), channel_id=1, source_target_pairs={{1,0},{3,2},{5,4},{7,6},{9,8},{11,10},{13,12},{15,14},{17,16},{19,... | collective-permute-start | bytes 884744 | tf_op jit(solution)/shard_map/ppermute | solution.py:22
  165.2 3.0 collective-permute-start.28
  166.9 4.2 %collective-permute-start.29 = (f32[1,192,128]{2,1,0:T(8,128)S(1)}, f32[1,192,128]{2,1,0:T(8,128)S(1)}, u32[]{:S(2)}, u32[]{:S(2)}) collective-permute-start(f32[1,192,128]{2,1,0:T(8,128)S(1)} %get-tuple-element.21), channel_id=1, source_target_pairs={{2,0},{4,2},{6,4},{8,6},{10,8},{12,10},{14,12},{16,14},{18,16},{20... | collective-permute-start | bytes 294920 | tf_op jit(solution)/shard_map/ppermute | solution.py:22
  171.7 7.1 %collective-permute-start.31 = (bf16[1,1,192,128]{3,2,1,0:T(8,128)(2,1)S(1)}, bf16[1,1,192,128]{3,2,1,0:T(8,128)(2,1)S(1)}, u32[]{:S(2)}, u32[]{:S(2)}) collective-permute-start(bf16[1,1,192,128]{3,2,1,0:T(8,128)(2,1)S(1)} %get-tuple-element.4), channel_id=1, source_target_pairs={{2,0},{4,2},{6,4},{8,6},{10,8},{12,10},{14,12},{16,14},{18,16},{20... | collective-permute-start | bytes 147464 | tf_op jit(solution)/shard_map/ppermute | solution.py:22
  173.0 6.6 %collective-permute-start.30 = (bf16[1,1,192,128]{3,2,1,0:T(8,128)(2,1)S(1)}, bf16[1,1,192,128]{3,2,1,0:T(8,128)(2,1)S(1)}, u32[]{:S(2)}, u32[]{:S(2)}) collective-permute-start(bf16[1,1,192,128]{3,2,1,0:T(8,128)(2,1)S(1)} %get-tuple-element.4), channel_id=1, source_target_pairs={{0,2},{2,4},{4,6},{6,8},{8,10},{10,12},{12,14},{14,16},{16,18},{18... | collective-permute-start | bytes 147464 | tf_op jit(solution)/shard_map/ppermute | solution.py:20
  179.7 7.6 %collective-permute-start.33 = (bf16[3,1,192,128]{3,2,1,0:T(8,128)(2,1)S(1)}, bf16[3,1,192,128]{3,2,1,0:T(8,128)(2,1)S(1)}, u32[]{:S(2)}, u32[]{:S(2)}) collective-permute-start(bf16[3,1,192,128]{3,2,1,0:T(8,128)(2,1)S(1)} %pad_maximum_fusion.7), channel_id=1, source_target_pairs={{1,0},{3,2},{5,4},{7,6},{9,8},{11,10},{13,12},{15,14},{17,16},{19,... | collective-permute-start | bytes 442376 | tf_op jit(solution)/shard_map/ppermute | solution.py:22
  181.0 8.0 %collective-permute-start.32 = (bf16[3,1,192,128]{3,2,1,0:T(8,128)(2,1)S(1)}, bf16[3,1,192,128]{3,2,1,0:T(8,128)(2,1)S(1)}, u32[]{:S(2)}, u32[]{:S(2)}) collective-permute-start(bf16[3,1,192,128]{3,2,1,0:T(8,128)(2,1)S(1)} %pad_maximum_fusion.7), channel_id=1, source_target_pairs={{0,1},{2,3},{4,5},{6,7},{8,9},{10,11},{12,13},{14,15},{16,17},{18,... | collective-permute-start | bytes 442376 | tf_op jit(solution)/shard_map/ppermute | solution.py:20
  199.2 11.6 %collective-permute-start.34 = (f32[3,1,192,128]{3,2,1,0:T(8,128)S(1)}, f32[3,1,192,128]{3,2,1,0:T(8,128)S(1)}, u32[]{:S(2)}, u32[]{:S(2)}) collective-permute-start(f32[3,1,192,128]{3,2,1,0:T(8,128)S(1)} %get-tuple-element.8), channel_id=1, source_target_pairs={{0,1},{2,3},{4,5},{6,7},{8,9},{10,11},{12,13},{14,15},{16,17},{18,... | collective-permute-start | bytes 884744 | tf_op jit(solution)/shard_map/ppermute | solution.py:20
  203.7 11.2 %collective-permute-start.35 = (f32[3,1,192,128]{3,2,1,0:T(8,128)S(1)}, f32[3,1,192,128]{3,2,1,0:T(8,128)S(1)}, u32[]{:S(2)}, u32[]{:S(2)}) collective-permute-start(f32[3,1,192,128]{3,2,1,0:T(8,128)S(1)} %get-tuple-element.9), channel_id=1, source_target_pairs={{1,0},{3,2},{5,4},{7,6},{9,8},{11,10},{13,12},{15,14},{17,16},{19,... | collective-permute-start | bytes 884744 | tf_op jit(solution)/shard_map/ppermute | solution.py:22
  215.1 2.8 collective-permute-start.36
  216.6 6.5 %collective-permute-start.37 = (f32[1,192,128]{2,1,0:T(8,128)S(1)}, f32[1,192,128]{2,1,0:T(8,128)S(1)}, u32[]{:S(2)}, u32[]{:S(2)}) collective-permute-start(f32[1,192,128]{2,1,0:T(8,128)S(1)} %get-tuple-element.19), channel_id=1, source_target_pairs={{2,0},{4,2},{6,4},{8,6},{10,8},{12,10},{14,12},{16,14},{18,16},{20... | collective-permute-start | bytes 294920 | tf_op jit(solution)/shard_map/ppermute | solution.py:22
  223.7 7.1 %collective-permute-start.39 = (f32[1,1,192,128]{3,2,1,0:T(8,128)S(1)}, f32[1,1,192,128]{3,2,1,0:T(8,128)S(1)}, u32[]{:S(2)}, u32[]{:S(2)}) collective-permute-start(f32[1,1,192,128]{3,2,1,0:T(8,128)S(1)} %get-tuple-element.15), channel_id=1, source_target_pairs={{2,0},{4,2},{6,4},{8,6},{10,8},{12,10},{14,12},{16,14},{18,16},{20... | collective-permute-start | bytes 294920 | tf_op jit(solution)/shard_map/ppermute | solution.py:22
  225.0 6.7 %collective-permute-start.38 = (f32[1,1,192,128]{3,2,1,0:T(8,128)S(1)}, f32[1,1,192,128]{3,2,1,0:T(8,128)S(1)}, u32[]{:S(2)}, u32[]{:S(2)}) collective-permute-start(f32[1,1,192,128]{3,2,1,0:T(8,128)S(1)} %get-tuple-element.15), channel_id=1, source_target_pairs={{0,2},{2,4},{4,6},{6,8},{8,10},{10,12},{12,14},{14,16},{16,18},{18... | collective-permute-start | bytes 294920 | tf_op jit(solution)/shard_map/ppermute | solution.py:20
  231.8 9.4 %collective-permute-start.41 = (f32[3,1,192,128]{3,2,1,0:T(8,128)S(1)}, f32[3,1,192,128]{3,2,1,0:T(8,128)S(1)}, u32[]{:S(2)}, u32[]{:S(2)}) collective-permute-start(f32[3,1,192,128]{3,2,1,0:T(8,128)S(1)} %pad_maximum_fusion.5), channel_id=1, source_target_pairs={{1,0},{3,2},{5,4},{7,6},{9,8},{11,10},{13,12},{15,14},{17,16},{19,... | collective-permute-start | bytes 884744 | tf_op jit(solution)/shard_map/ppermute | solution.py:22
  233.1 9.9 %collective-permute-start.40 = (f32[3,1,192,128]{3,2,1,0:T(8,128)S(1)}, f32[3,1,192,128]{3,2,1,0:T(8,128)S(1)}, u32[]{:S(2)}, u32[]{:S(2)}) collective-permute-start(f32[3,1,192,128]{3,2,1,0:T(8,128)S(1)} %pad_maximum_fusion.5), channel_id=1, source_target_pairs={{0,1},{2,3},{4,5},{6,7},{8,9},{10,11},{12,13},{14,15},{16,17},{18,... | collective-permute-start | bytes 884744 | tf_op jit(solution)/shard_map/ppermute | solution.py:20
  245.3 44.0 %copy-start.5 = (f32[16,1,24,48]{3,2,1,0:T(8,128)S(1)}, f32[16,1,24,48]{3,2,1,0:T(8,128)}, u32[]{:S(2)}) copy-start(f32[16,1,24,48]{3,2,1,0:T(8,128)} %param.14) | copy-start | bytes 221188
  245.3 55.8 %copy-start.2 = (f32[768,128]{1,0:T(8,128)S(1)}, f32[768,128]{1,0:T(8,128)}, u32[]{:S(2)}) copy-start(f32[768,128]{1,0:T(8,128)} %gather_fusion.5) | copy-start | bytes 1179652
  247.7 6.0 %collective-permute-start.42 = (f32[3,1,24,128]{3,2,1,0:T(8,128)S(1)}, f32[3,1,24,128]{3,2,1,0:T(8,128)S(1)}, u32[]{:S(2)}, u32[]{:S(2)}) collective-permute-start(f32[3,1,24,128]{3,2,1,0:T(8,128)S(1)} %get-tuple-element.24), channel_id=1, source_target_pairs={{0,1},{2,3},{4,5},{6,7},{8,9},{10,11},{12,13},{14,15},{16,17},{18,... | collective-permute-start | bytes 110600 | tf_op jit(solution)/shard_map/ppermute | solution.py:20
  252.1 5.9 %collective-permute-start.43 = (f32[3,1,24,128]{3,2,1,0:T(8,128)S(1)}, f32[3,1,24,128]{3,2,1,0:T(8,128)S(1)}, u32[]{:S(2)}, u32[]{:S(2)}) collective-permute-start(f32[3,1,24,128]{3,2,1,0:T(8,128)S(1)} %get-tuple-element.25), channel_id=1, source_target_pairs={{1,0},{3,2},{5,4},{7,6},{9,8},{11,10},{13,12},{15,14},{17,16},{19,... | collective-permute-start | bytes 110600 | tf_op jit(solution)/shard_map/ppermute | solution.py:22
  258.0 3.7 %collective-permute-start.44 = (f32[1,24,128]{2,1,0:T(8,128)S(1)}, f32[1,24,128]{2,1,0:T(8,128)S(1)}, u32[]{:S(2)}, u32[]{:S(2)}) collective-permute-start(f32[1,24,128]{2,1,0:T(8,128)S(1)} %get-tuple-element.28), channel_id=1, source_target_pairs={{0,2},{2,4},{4,6},{6,8},{8,10},{10,12},{12,14},{14,16},{16,18},{18... | collective-permute-start | bytes 36872 | tf_op jit(solution)/shard_map/ppermute | solution.py:20
  260.4 8.8 %collective-permute-start.45 = (f32[1,24,128]{2,1,0:T(8,128)S(1)}, f32[1,24,128]{2,1,0:T(8,128)S(1)}, u32[]{:S(2)}, u32[]{:S(2)}) collective-permute-start(f32[1,24,128]{2,1,0:T(8,128)S(1)} %get-tuple-element.29), channel_id=1, source_target_pairs={{2,0},{4,2},{6,4},{8,6},{10,8},{12,10},{14,12},{16,14},{18,16},{20... | collective-permute-start | bytes 36872 | tf_op jit(solution)/shard_map/ppermute | solution.py:22
  296.6 5.4 %collective-permute-start.47 = (bf16[1,48,128]{2,1,0:T(8,128)(2,1)S(1)}, bf16[1,48,128]{2,1,0:T(8,128)(2,1)S(1)}, u32[]{:S(2)}, u32[]{:S(2)}) collective-permute-start(bf16[1,48,128]{2,1,0:T(8,128)(2,1)S(1)} %bitcast.252), channel_id=1, source_target_pairs={{2,0},{4,2},{6,4},{8,6},{10,8},{12,10},{14,12},{16,14},{18,16},{20... | collective-permute-start | bytes 36872 | tf_op jit(solution)/shard_map/ppermute | solution.py:22
  297.8 4.1 %collective-permute-start.46 = (bf16[1,48,128]{2,1,0:T(8,128)(2,1)S(1)}, bf16[1,48,128]{2,1,0:T(8,128)(2,1)S(1)}, u32[]{:S(2)}, u32[]{:S(2)}) collective-permute-start(bf16[1,48,128]{2,1,0:T(8,128)(2,1)S(1)} %bitcast.253), channel_id=1, source_target_pairs={{0,2},{2,4},{4,6},{6,8},{8,10},{10,12},{12,14},{14,16},{16,18},{18... | collective-permute-start | bytes 36872 | tf_op jit(solution)/shard_map/ppermute | solution.py:20
  309.6 20.0 %copy-start.7 = (f32[192,128]{1,0:T(8,128)S(1)}, f32[192,128]{1,0:T(8,128)}, u32[]{:S(2)}) copy-start(f32[192,128]{1,0:T(8,128)} %get-tuple-element.5) | copy-start | bytes 294916
  309.6 10.7 %collective-permute-start.48 = (f32[3,1,192,128]{3,2,1,0:T(8,128)S(1)}, f32[3,1,192,128]{3,2,1,0:T(8,128)S(1)}, u32[]{:S(2)}, u32[]{:S(2)}) collective-permute-start(f32[3,1,192,128]{3,2,1,0:T(8,128)S(1)} %get-tuple-element.6), channel_id=1, source_target_pairs={{0,1},{2,3},{4,5},{6,7},{8,9},{10,11},{12,13},{14,15},{16,17},{18,... | collective-permute-start | bytes 884744 | tf_op jit(solution)/shard_map/ppermute | solution.py:20
  313.8 10.7 %collective-permute-start.49 = (f32[3,1,192,128]{3,2,1,0:T(8,128)S(1)}, f32[3,1,192,128]{3,2,1,0:T(8,128)S(1)}, u32[]{:S(2)}, u32[]{:S(2)}) collective-permute-start(f32[3,1,192,128]{3,2,1,0:T(8,128)S(1)} %get-tuple-element.7), channel_id=1, source_target_pairs={{1,0},{3,2},{5,4},{7,6},{9,8},{11,10},{13,12},{15,14},{17,16},{19,... | collective-permute-start | bytes 884744 | tf_op jit(solution)/shard_map/ppermute | solution.py:22
  324.6 2.6 collective-permute-start.50
  325.9 3.7 %collective-permute-start.51 = (f32[1,192,128]{2,1,0:T(8,128)S(1)}, f32[1,192,128]{2,1,0:T(8,128)S(1)}, u32[]{:S(2)}, u32[]{:S(2)}) collective-permute-start(f32[1,192,128]{2,1,0:T(8,128)S(1)} %get-tuple-element.17), channel_id=1, source_target_pairs={{2,0},{4,2},{6,4},{8,6},{10,8},{12,10},{14,12},{16,14},{18,16},{20... | collective-permute-start | bytes 294920 | tf_op jit(solution)/shard_map/ppermute | solution.py:22
where the time goes:
time: 334 us; the launch traced here: 330 us
  starting transfers between devices  130 us (39%)
  waiting for transfers between devices  79.8 us (24%)
  blocking collectives  54.4 us (16%)
  other arithmetic  38.9 us (12%)
  local copies, waits for them, and re-layouts  18.3 us (5%)
  matrix products  6.13 us (2%)
    ppermute x26, starting transfers between devices, extended(): lax.ppermute(tail, axis, [(i, (i + 1) % count) for i in range(ends)])  96.7 us
    ppermute x26, waiting for transfers between devices, extended(): lax.ppermute(head, axis, [((i + 1) % count, i) for i in range(ends)])  52.5 us
    all_gather x2, blocking collectives, body(): lax.all_gather(coarse_owned, 'row', axis=0, tiled=True)  40.7 us
    ppermute x26, starting transfers between devices, extended(): lax.ppermute(head, axis, [((i + 1) % count, i) for i in range(ends)])  33.5 us
    scatter-add x7, other arithmetic, spread_back(): jax.ops.segment_sum(values, target, num_segments=window_size + 1)  32.5 us
    ppermute x26, waiting for transfers between devices, extended(): lax.ppermute(tail, axis, [(i, (i + 1) % count) for i in range(ends)])  27.3 us
    psum x2, blocking collectives, body(): totals = lax.psum(coarse_part, 'col').astype(jnp.bfloat16)  13.7 us
    gather x6, local copies, waits for them, and re-layouts, take_rows(): picked = jnp.take(window_rows, positions, axis=0, mode='clip')  9 us
  transfers between devices with their start and end apart: 52, of which 27 were waited for; matrix products, arithmetic and copies ran while one was open for 7% of the time, Pallas kernels for 0%

commit v1 on v0

v1 whole, which is shorter than its diff:
```python
import functools

import jax
import jax.numpy as jnp
from jax import lax
from jax.experimental import pallas as pl
from jax.experimental.pallas import tpu as pltpu
from jax.sharding import PartitionSpec as P

ITERS = 2
BF = jnp.bfloat16
F32 = jnp.float32
MESH_ID = pl.DeviceIdType.MESH
NT = (((1,), (1,)), ((), ()))


def mm(a, b):
    return jnp.dot(a, b, preferred_element_type=F32)


def kernel(
    R, C, B,
    k_hbm, m_hbm, basis_ref, loads_ref, start_ref, panel_ref, sizes_ref, ids_ref, cids_ref,
    x_out, r_out,
    kv, mv, s_ref, st_ref, t_ref, am_ref, a_ref, pbw_ref, bpw_ref, lw_ref,
    idw, xw, rw, psend, precv, usend, urecv, csend, crecv, cw, g_ref, loc_ref, inv_ref,
    ld_sem, s_id, r_id, s_x, r_x, s_r, r_r, s_p, r_p, s_u, r_u, s_c, r_c, s_w, r_w,
    s_g1, r_g1, s_g2, r_g2,
):
    A = R // B
    W = 2 if C == 2 else 3
    NB = 3 * W
    own_k = 0 if W == 2 else 1
    own = W + own_k
    OWN, COLS = start_ref.shape
    NI = ids_ref.shape[1]
    NCD = csend.shape[2]
    r = lax.axis_index("row")
    c = lax.axis_index("col")
    ra = r // B
    rb = r % B

    copy_k = pltpu.make_async_copy(k_hbm, kv, ld_sem.at[0])
    copy_m = pltpu.make_async_copy(m_hbm, mv, ld_sem.at[1])
    copy_k.start()
    copy_m.start()

    def both(x, y):
        if x is None:
            return y
        return x if y is None else jnp.logical_and(x, y)

    def row_ok(d):
        return None if d == 1 else (r > 0 if d == 0 else r < R - 1)

    def col_of(k):
        if W == 2:
            return c if k == 0 else 1 - c
        return c + (k - 1)

    def col_ok(k):
        if W == 2 or k == 1:
            return None
        return c > 0 if k == 0 else c < C - 1

    def mirror(b):
        d, k = b // W, b % W
        return (2 - d) * W + (k if W == 2 else 2 - k)

    nbrs = [b for b in range(NB) if b != own]
    oks = {b: both(row_ok(b // W), col_ok(b % W)) for b in nbrs}
    target = {b: (r + (b // W - 1), col_of(b % W)) for b in nbrs}

    def guarded(ok, fn):
        if ok is None:
            fn()
        else:
            pl.when(ok)(fn)

    def unless(ok, fn):
        if ok is not None:
            pl.when(jnp.logical_not(ok))(fn)

    def remote(src, dst, ss, rs, dev):
        return pltpu.make_async_remote_copy(
            src_ref=src, dst_ref=dst, send_sem=ss, recv_sem=rs,
            device_id=dev, device_id_type=MESH_ID,
        )

    finals = []

    def send_all(make):
        for b in nbrs:
            desc = make(b)
            guarded(oks[b], desc.start)
            finals.append((oks[b], desc.wait_send))

    g1 = [(((ra + i) % A) * B + rb, c) for i in range(A)]
    g2 = {(j, i): (ra * B + (rb + i) % B, (c + j) % C) for j in range(C) for i in range(B)}
    pan = {(d, j): (r + d - 1, (c + j) % C) for d in range(3) for j in range(C) if (d, j) != (1, 0)}

    barrier = pltpu.get_barrier_semaphore()

    def signal(dev):
        pl.semaphore_signal(barrier, inc=1, device_id=dev, device_id_type=MESH_ID)

    for b in nbrs:
        guarded(oks[b], functools.partial(signal, target[b]))
    for i in range(1, A):
        signal(g1[i])
    for key, dev in g2.items():
        if key != (0, 0):
            signal(dev)
    if C > 2:
        for (d, j), dev in pan.items():
            guarded(row_ok(d), functools.partial(signal, dev))

    def floor_div(x, n):
        return jnp.floor((x + 0.5) * (1.0 / n))

    ids_i = ids_ref[...]
    live = lax.broadcasted_iota(jnp.int32, (1, NI), 1) < sizes_ref[0]
    idw[own] = jnp.where(live, ids_i, -1)
    ids_f = ids_i.astype(F32)
    owner = floor_div(ids_f, OWN)
    orow = floor_div(owner, C)
    ocol = owner - orow * C
    rf = r.astype(F32)
    cf = c.astype(F32)
    kslot = jnp.abs(ocol - cf) if W == 2 else ocol - cf + 1.0
    pos_f = ((orow - rf + 1.0) * W + kslot) * OWN + (ids_f - owner * OWN)
    pos = jnp.where(live, pos_f, -1.0).astype(jnp.int32)
    xw[0, own] = start_ref[...].astype(BF)

    for b in nbrs:
        def fill(b=b):
            idw[b] = jnp.full((1, NI), -1, jnp.int32)
            for s in range(ITERS):
                xw[s, b] = jnp.zeros((OWN, COLS), BF)
                rw[s, b] = jnp.zeros((OWN, COLS), BF)
        unless(oks[b], fill)
    for d in (0, 2):
        def fill_c(d=d):
            for j in range(C):
                cw[j, d] = jnp.zeros(cw.shape[2:], BF)
        unless(row_ok(d), fill_c)
    cw[c, 1] = panel_ref[...]

    amount = (A - 1) + (C * B - 1)
    conds = [oks[b] for b in nbrs]
    if C > 2:
        conds += [row_ok(d) for d, j in pan]
    for ok in conds:
        amount = amount + (1 if ok is None else ok.astype(jnp.int32))
    pl.semaphore_wait(barrier, amount)

    def send_x(s):
        send_all(lambda b: remote(
            xw.at[s, own], xw.at[s, mirror(b)], s_x.at[s, b], r_x.at[s, mirror(b)], target[b]))

    send_x(0)
    send_all(lambda b: remote(
        idw.at[own], idw.at[mirror(b)], s_id.at[b], r_id.at[mirror(b)], target[b]))

    pos_col = jnp.transpose(jnp.broadcast_to(pos, (128, NI)))
    WN = NB * OWN
    for j in range(0, WN, 128):
        n = min(128, WN - j)
        lane = lax.broadcasted_iota(jnp.int32, (NI, 128), 1) + j
        hot = jnp.where(lane == pos_col, 1.0, 0.0).astype(BF)
        s_ref[:, j:j + n] = hot[:, :n]
    for b in range(NB):
        sub = lax.broadcasted_iota(jnp.int32, (OWN, NI), 0) + b * OWN
        st_ref[b * OWN:(b + 1) * OWN, :] = jnp.where(sub == pos, 1.0, 0.0).astype(BF)

    def by_rows(rows, fn):
        def step(i, carry):
            fn(pl.ds(pl.multiple_of(i * OWN, OWN), OWN))
            return carry
        lax.fori_loop(0, rows // OWN, step, 0)

    def times_s(src, dst):
        def one(at):
            dst[at, :] = mm(src[at, :], s_ref[...]).astype(BF)
        by_rows(NI, one)

    def st_times(src, dst):
        def one(at):
            dst[at, :] = mm(st_ref[at, :], src[...]).astype(dst.dtype)
        by_rows(WN, one)

    def recv(dst, sem):
        return remote(dst, dst, sem, sem, (r, c)).wait_recv

    copy_k.wait()
    times_s(kv, t_ref)
    st_times(loads_ref, lw_ref)
    st_times(t_ref, a_ref)

    inv = None
    x_now = start_ref[...]
    for s in range(ITERS):
        for b in nbrs:
            guarded(oks[b], recv(xw.at[s, b], r_x.at[s, b]))
        x_all = xw[s].reshape(WN, COLS)
        for b in nbrs + [own]:
            at = slice(b * OWN, (b + 1) * OWN)
            part = lw_ref[at, :].astype(F32) - mm(a_ref[at, :], x_all)
            if b == own:
                r_out[...] = part
            else:
                psend[s, b] = part.astype(BF)
                desc = remote(psend.at[s, b], precv.at[s, mirror(b)], s_p.at[s, b],
                              r_p.at[s, mirror(b)], target[b])
                guarded(oks[b], desc.start)
                finals.append((oks[b], desc.wait_send))
        if s == 0:
            for (d, j), dev in pan.items():
                desc = remote(panel_ref, cw.at[c, 2 - d], s_w.at[d, j], r_w.at[2 - d, j], dev)
                guarded(row_ok(d), desc.start)
                finals.append((row_ok(d), desc.wait_send))
            for b in nbrs:
                guarded(oks[b], recv(idw.at[b], r_id.at[b]))
            mine = lax.broadcasted_iota(jnp.int32, (OWN, 128), 0) + (r * C + c) * OWN
            acc = jnp.zeros((OWN, 128), F32)
            for b in range(NB):
                for j in range(0, NI, 128):
                    acc = acc + jnp.where(idw[b, :, j:j + 128] == mine, 1.0, 0.0)
            count = jnp.sum(acc, axis=1, keepdims=True)
            inv_ref[...] = jnp.broadcast_to(1.0 / jnp.maximum(count, 1.0), (OWN, COLS))

            cf_ids = cids_ref[...].astype(F32)
            cpos = (cf_ids - (rf - 1.0) * (C * NCD)).astype(jnp.int32)
            n_c = 3 * C * NCD
            pt = jnp.where(
                lax.broadcasted_iota(jnp.int32, (n_c, cpos.shape[1]), 0) == cpos, 1.0, 0.0
            ).astype(BF)
            basis = basis_ref[...]
            pb = lax.dot_general(pt, basis, NT, preferred_element_type=F32).astype(BF)
            bp = lax.dot_general(basis, pt, NT, preferred_element_type=F32).astype(BF)
            pbw_ref[...] = mm(pb, s_ref[...]).astype(BF)
            by_rows(WN, lambda at: bpw_ref.__setitem__((at, slice(None)), mm(st_ref[at, :], bp).astype(BF)))
            copy_m.wait()
            times_s(mv, t_ref)
        for b in nbrs:
            guarded(oks[b], recv(precv.at[s, b], r_p.at[s, b]))

            def add(b=b):
                r_out[...] = r_out[...] + precv[s, b].astype(F32)
            guarded(oks[b], add)
        rw[s, own] = (inv_ref[...] * r_out[...]).astype(BF)
        send_all(lambda b: remote(
            rw.at[s, own], rw.at[s, mirror(b)], s_r.at[s, b], r_r.at[s, mirror(b)], target[b]))
        if s == 0:
            st_times(t_ref, am_ref)
        for b in nbrs:
            guarded(oks[b], recv(rw.at[s, b], r_r.at[s, b]))
        r_all = rw[s].reshape(WN, COLS)
        csend[s] = mm(pbw_ref[...], r_all).reshape(csend.shape[1:])
        send_all(lambda b: remote(
            csend.at[s, (b // W) * C + target[b][1]], crecv.at[s, mirror(b)],
            s_c.at[s, b], r_c.at[s, mirror(b)], target[b]))
        crecv[s, own] = csend[s, C + c]

        def local(at):
            loc_ref[at, :] = mm(am_ref[at, :], rw[s].reshape(WN, COLS))
        by_rows(WN, local)
        for b in nbrs:
            guarded(oks[b], recv(crecv.at[s, b], r_c.at[s, b]))

            def add_c(b=b):
                crecv[s, own] = crecv[s, own] + crecv[s, b]
            guarded(oks[b], add_c)
        g_ref[s, c, rb, ra] = crecv[s, own].astype(BF)
        for i in range(1, A):
            at = g_ref.at[s, c, rb, ra]
            desc = remote(at, at, s_g1.at[s, i], r_g1.at[s, i], g1[i])
            desc.start()
            finals.append((None, desc.wait_send))
        for i in range(1, A):
            recv(g_ref.at[s, c, rb, (ra + A - i) % A], r_g1.at[s, i])()
        for (j, i), dev in g2.items():
            if (j, i) == (0, 0):
                continue
            at = g_ref.at[s, c, rb]
            desc = remote(at, at, s_g2.at[s, j, i], r_g2.at[s, j, i], dev)
            desc.start()
            finals.append((None, desc.wait_send))
        for (j, i) in g2:
            if (j, i) == (0, 0):
                continue
            recv(g_ref.at[s, (c + C - j) % C, (rb + B - i) % B], r_g2.at[s, j, i])()
        if s == 0:
            for (d, j) in pan:
                guarded(row_ok(d), recv(cw.at[(c + C - j) % C, d], r_w.at[d, j]))
        sol = None
        for j in range(C):
            rhs = g_ref[s, j].astype(F32).reshape(R * NCD, COLS).astype(BF)
            term = mm(cw[j].reshape(3 * cw.shape[2], R * NCD), rhs)
            sol = term if sol is None else sol + term
        sol = sol.astype(BF)
        x_out[...] = x_now
        for b in nbrs + [own]:
            at = slice(b * OWN, (b + 1) * OWN)
            upd = loc_ref[at, :] + mm(bpw_ref[at, :], sol)
            if b == own:
                loc_ref[at, :] = upd
            else:
                usend[s, b] = upd.astype(BF)
                desc = remote(usend.at[s, b], urecv.at[s, mirror(b)], s_u.at[s, b],
                              r_u.at[s, mirror(b)], target[b])
                guarded(oks[b], desc.start)
                finals.append((oks[b], desc.wait_send))
        mine_at = slice(own * OWN, (own + 1) * OWN)
        for b in nbrs:
            guarded(oks[b], recv(urecv.at[s, b], r_u.at[s, b]))

            def add_u(b=b):
                loc_ref[mine_at, :] = loc_ref[mine_at, :] + urecv[s, b].astype(F32)
            guarded(oks[b], add_u)
        x_now = x_out[...] + inv_ref[...] * loc_ref[mine_at, :]
        x_out[...] = x_now
        if s + 1 < ITERS:
            xw[s + 1, own] = x_now.astype(BF)
            send_x(s + 1)
    for ok, fn in finals:
        guarded(ok, fn)


def solution(mesh):
    R, C = mesh.shape["row"], mesh.shape["col"]
    B = 4 if R % 4 == 0 else (2 if R % 2 == 0 else 1)
    A = R // B
    W = 2 if C == 2 else 3
    NB = 3 * W

    def body(stiffness, local_inverse, averaging_basis, loads, start, coarse_inverse, sizes,
             dof_ids, coarse_ids):
        OWN, COLS = start.shape
        NI = dof_ids.shape[1]
        NCD, NR = coarse_inverse.shape[2:]
        WN = NB * OWN
        panel = coarse_inverse.reshape(A, B, NCD, NR).transpose(3, 1, 0, 2)
        panel = panel.reshape(NR, R * NCD).astype(BF)
        V = pltpu.VMEM
        D = pltpu.SemaphoreType.DMA
        S = ITERS
        vm = pl.BlockSpec(memory_space=pltpu.VMEM)
        hb = pl.BlockSpec(memory_space=pl.ANY)
        sm = pl.BlockSpec(memory_space=pltpu.SMEM)
        n_c = 3 * C * NCD
        return pl.pallas_call(
            functools.partial(kernel, R, C, B),
            out_shape=(jax.ShapeDtypeStruct((OWN, COLS), F32),) * 2,
            in_specs=[hb, hb, vm, vm, vm, vm, sm, vm, vm],
            out_specs=(vm, vm),
            scratch_shapes=[
                V((NI, NI), BF), V((NI, NI), BF), V((NI, WN), BF), V((WN, NI), BF),
                V((NI, WN), BF), V((WN, WN), BF), V((WN, WN), BF),
                V((n_c, WN), BF), V((WN, n_c), BF), V((WN, COLS), BF),
                V((NB, 1, NI), jnp.int32), V((S, NB, OWN, COLS), BF), V((S, NB, OWN, COLS), BF),
                V((S, NB, OWN, COLS), BF), V((S, NB, OWN, COLS), BF),
                V((S, NB, OWN, COLS), BF), V((S, NB, OWN, COLS), BF),
                V((S, 3 * C, NCD, COLS), F32), V((S, NB, NCD, COLS), F32),
                V((C, 3, NR, R * NCD), BF), V((S, C, B, A, NCD, COLS), BF),
                V((WN, COLS), F32), V((OWN, COLS), F32),
                D((2,)), D((NB,)), D((NB,)), D((S, NB)), D((S, NB)), D((S, NB)), D((S, NB)),
                D((S, NB)), D((S, NB)), D((S, NB)), D((S, NB)), D((S, NB)), D((S, NB)),
                D((3, C)), D((3, C)), D((S, A)), D((S, A)), D((S, C, B)), D((S, C, B)),
            ],
            compiler_params=pltpu.CompilerParams(
                collective_id=0, has_side_effects=True, vmem_limit_bytes=62 << 20
            ),
        )(stiffness[0], local_inverse[0], averaging_basis[0], loads[0], start, panel, sizes,
          dof_ids, coarse_ids)

    in_specs = (
        P(("row", "col"), None, None),
        P(("row", "col"), None, None),
        P(("row", "col"), None, None),
        P(("row", "col"), None, None),
        P(("row", "col"), None),
        P(None, "col", None, "row"),
        P(("row", "col")),
        P(("row", "col"), None),
        P(("row", "col"), None),
    )
    out_specs = (P(("row", "col"), None), P(("row", "col"), None))
    return jax.shard_map(body, mesh=mesh, in_specs=in_specs, out_specs=out_specs, check_vma=False)
```

time: 334 us -> 83.1 us (0.25)
  starting transfers between devices: 130 us -> 0 us
  waiting for transfers between devices: 79.8 us -> 0 us
  Pallas kernels: 0 us -> 74.9 us
  blocking collectives: 54.4 us -> 0 us
  other arithmetic: 38.9 us -> 0.94 us
  local copies, waits for them, and re-layouts: 18.3 us -> 5.5 us
  matrix products: 6.13 us -> 0 us
    ppermute x52 -> x0, starting transfers between devices: 130 us -> none  [the longest x26 96.7 us: extended(): lax.ppermute(tail, axis, [(i, (i + 1) % count) for i in range(ends)])]
    ppermute x52 -> x0, waiting for transfers between devices: 79.8 us -> none  [the longest x26 52.5 us: extended(): lax.ppermute(head, axis, [((i + 1) % count, i) for i in range(ends)])]
    pallas_call x0 -> x1, Pallas kernels: none -> 74.9 us  [body(): pl.pallas_call(functools.partial(kernel, R, C, B), out_shape=(jax.ShapeDt...]
    all_gather x2 -> x0, blocking collectives: 40.7 us -> none  [body(): lax.all_gather(coarse_owned, 'row', axis=0, tiled=True)]
    scatter-add x7 -> x0, other arithmetic: 32.5 us -> none  [spread_back(): jax.ops.segment_sum(values, target, num_segments=window_size + 1)]
    psum x2 -> x0, blocking collectives: 13.7 us -> none  [body(): totals = lax.psum(coarse_part, 'col').astype(jnp.bfloat16)]
    gather x7 -> x0, local copies, waits for them, and re-layouts: 13.5 us -> none  [the longest x6 9 us: take_rows(): picked = jnp.take(window_rows, positions, axis=0, mode='clip')]
    dot_general x10 -> x0, matrix products: 6.13 us -> none  [the longest x2 1.86 us: body(): lax.dot_general(averaging_basis[0], scaled, (((0,), (0,)), ((), ())), pre...]
  transfers between devices with their start and end apart: 52 -> 0, of which waited for: 27 -> 0; matrix products, arithmetic and copies ran while one was open for 7% -> 0% of each run, Pallas kernels for 0% -> 0%
where the time goes in v1:
time: 83.1 us; the launch traced here: 82.6 us
  Pallas kernels  74.9 us (90%)
  local copies, waits for them, and re-layouts  5.5 us (7%)
  between operations  1.3 us (2%)
  other arithmetic  0.94 us (1%)
    pallas_call x1, Pallas kernels, body(): pl.pallas_call(functools.partial(kernel, R, C, B), out_shape=(jax.ShapeDt...  74.9 us
    unnamed x3, local copies, waits for them, and re-layouts  4.78 us

profile of v1, /device:TPU:0, one launch (start us, length us, event | category | flops | bytes accessed | tf_op | source)
XLA Modules:
  0.0 82.6 jit_solution(5498652784681435401)
XLA Ops:
  1.3 0.9 %convert_element_type.9 = bf16[16,1,24,48]{3,2,1,0:T(8,128)(2,1)S(1)} convert(f32[16,1,24,48]{3,2,1,0:T(8,128)} %param.14) | non-fusion elementwise | flops 18432 | bytes 110592 | tf_op jit(solution)/shard_map/convert_element_type | solution.py:344
  2.2 0.7 copy.15.panel_ref
  2.9 1.7 %copy.13 = bf16[1,768,64]{2,1,0:T(8,128)(2,1)} copy(bf16[1,768,64]{1,2,0:T(8,128)(2,1)} %param.11) | data formatting | bytes 196608 | tf_op args[2]
  4.7 74.9 %shard_map.104 = (f32[192,128]{1,0:T(8,128)}, f32[192,128]{1,0:T(8,128)}) custom-call(bf16[768,768]{1,0:T(8,128)(2,1)} %bitcast.8, bf16[768,768]{1,0:T(8,128)(2,1)} %bitcast.9, bf16[768,64]{1,0:T(8,128)(2,1)} %bitcast.10, bf16[768,128]{1,0:T(8,128)(2,1)} %bitcast.13, f32[192,128]{1,0:T(8,128)} %start_ref.1, bf16[48,384]{1,0:T(8,128)(2,1)} %copy.15.panel_ref, ...), custom_call_target="tpu_custom_call" | custom-call | tf_op jit(solution)/shard_map/pallas_call | solution.py:352
  79.5 1.5 %copy.19 = f32[192,128]{1,0:T(8,128)} copy(f32[192,128]{1,0:T(8,128)} %get-tuple-element.4) | data formatting | bytes 196608
  81.1 1.5 %copy.20 = f32[192,128]{1,0:T(8,128)} copy(f32[192,128]{1,0:T(8,128)} %get-tuple-element.5) | data formatting | bytes 196608
  (1 shorter events, 0.0 us)

commit v2 on v1

v2 whole, which is shorter than its diff:
```python
import functools

import jax
import jax.numpy as jnp
from jax import lax
from jax.experimental import pallas as pl
from jax.experimental.pallas import tpu as pltpu
from jax.sharding import PartitionSpec as P

ITERS = 2
BF = jnp.bfloat16
F32 = jnp.float32
MESH_ID = pl.DeviceIdType.MESH
NT = (((1,), (1,)), ((), ()))


def mm(a, b):
    return jnp.dot(a, b, preferred_element_type=F32)


def kernel(
    R, C, B,
    k_hbm, m_hbm, basis_ref, loads_ref, start_ref, panel_ref, sizes_ref, ids_ref, cids_ref,
    x_out, r_out,
    kv, mv, s_ref, st_ref, t_ref, t2_ref, tv_ref, tl_ref, pbs, pbr, qt,
    idw, xw, rw, psend, precv, usend, urecv, csend, crecv, cw, pan_ref, g_ref, inv_ref, acc_ref,
    ld_sem, s_id, r_id, s_x, r_x, s_r, r_r, s_p, r_p, s_u, r_u, s_b, r_b, s_c, r_c, s_w, r_w,
    s_g1, r_g1, s_g2, r_g2,
):
    A = R // B
    W = 2 if C == 2 else 3
    NB = 3 * W
    own_k = 0 if W == 2 else 1
    own = W + own_k
    OWN, COLS = start_ref.shape
    NI = ids_ref.shape[1]
    NCD, NR = panel_ref.shape[1:]
    n_c = 3 * NR
    r = lax.axis_index("row")
    c = lax.axis_index("col")
    ra = r // B
    rb = r % B

    copy_k = pltpu.make_async_copy(k_hbm, kv, ld_sem.at[0])
    copy_m = pltpu.make_async_copy(m_hbm, mv, ld_sem.at[1])
    copy_k.start()
    copy_m.start()

    def both(x, y):
        if x is None:
            return y
        return x if y is None else jnp.logical_and(x, y)

    def row_ok(d):
        return None if d == 1 else (r > 0 if d == 0 else r < R - 1)

    def row_ok5(e):
        if e == 2:
            return None
        return r >= 2 - e if e < 2 else r < R - (e - 2)

    def col_of(k):
        if W == 2:
            return c if k == 0 else 1 - c
        return c + (k - 1)

    def col_ok(k):
        if W == 2 or k == 1:
            return None
        return c > 0 if k == 0 else c < C - 1

    def mirror(b):
        d, k = b // W, b % W
        return (2 - d) * W + (k if W == 2 else 2 - k)

    nbrs = [b for b in range(NB) if b != own]
    oks = {b: both(row_ok(b // W), col_ok(b % W)) for b in nbrs}
    target = {b: (r + (b // W - 1), col_of(b % W)) for b in nbrs}

    def guarded(ok, fn):
        if ok is None:
            fn()
        else:
            pl.when(ok)(fn)

    def unless(ok, fn):
        if ok is not None:
            pl.when(jnp.logical_not(ok))(fn)

    def remote(src, dst, ss, rs, dev):
        return pltpu.make_async_remote_copy(
            src_ref=src, dst_ref=dst, send_sem=ss, recv_sem=rs,
            device_id=dev, device_id_type=MESH_ID,
        )

    finals = []

    def send_all(make):
        for b in nbrs:
            desc = make(b)
            guarded(oks[b], desc.start)
            finals.append((oks[b], desc.wait_send))

    g1 = [(((ra + i) % A) * B + rb, c) for i in range(A)]
    g2 = {(j, i): (ra * B + (rb + i) % B, (c + j) % C) for j in range(C) for i in range(B)}
    far = {(e, j): (r + (e - 2), (c + j) % C) for e in range(5) for j in range(C)
           if (e, j) != (2, 0)}

    barrier = pltpu.get_barrier_semaphore()

    def signal(dev):
        pl.semaphore_signal(barrier, inc=1, device_id=dev, device_id_type=MESH_ID)

    for (e, j), dev in far.items():
        guarded(row_ok5(e), functools.partial(signal, dev))
    for i in range(1, A):
        signal(g1[i])
    for key, dev in g2.items():
        if key != (0, 0):
            signal(dev)

    def floor_div(x, n):
        return jnp.floor((x + 0.5) * (1.0 / n))

    ids_i = ids_ref[...]
    live = lax.broadcasted_iota(jnp.int32, (1, NI), 1) < sizes_ref[0]
    idw[own] = jnp.where(live, ids_i, -1)
    ids_f = ids_i.astype(F32)
    owner = floor_div(ids_f, OWN)
    orow = floor_div(owner, C)
    ocol = owner - orow * C
    rf = r.astype(F32)
    cf = c.astype(F32)
    kslot = jnp.abs(ocol - cf) if W == 2 else ocol - cf + 1.0
    pos_f = ((orow - rf + 1.0) * W + kslot) * OWN + (ids_f - owner * OWN)
    pos = jnp.where(live, pos_f, -1.0).astype(jnp.int32)
    xw[0, own] = start_ref[...].astype(BF)

    for b in nbrs:
        def fill(b=b):
            idw[b] = jnp.full((1, NI), -1, jnp.int32)
            for s in range(ITERS):
                xw[s, b] = jnp.zeros((OWN, COLS), BF)
                rw[s, b] = jnp.zeros((OWN, COLS), BF)
            pbr[b] = jnp.zeros((n_c, OWN), BF)
        unless(oks[b], fill)
    for e in (0, 1, 3, 4):
        def fill_c(e=e):
            for j in range(C):
                cw[j, e] = jnp.zeros(cw.shape[2:], BF)
        unless(row_ok5(e), fill_c)

    amount = (A - 1) + (C * B - 1)
    for e, j in far:
        ok = row_ok5(e)
        amount = amount + (1 if ok is None else ok.astype(jnp.int32))
    pl.semaphore_wait(barrier, amount)

    def send_x(s):
        send_all(lambda b: remote(
            xw.at[s, own], xw.at[s, mirror(b)], s_x.at[s, b], r_x.at[s, mirror(b)], target[b]))

    send_x(0)
    send_all(lambda b: remote(
        idw.at[own], idw.at[mirror(b)], s_id.at[b], r_id.at[mirror(b)], target[b]))

    pos_col = jnp.transpose(jnp.broadcast_to(pos, (128, NI)))
    WN = NB * OWN
    for j in range(0, WN, 128):
        n = min(128, WN - j)
        lane = lax.broadcasted_iota(jnp.int32, (NI, 128), 1) + j
        hot = jnp.where(lane == pos_col, 1.0, 0.0).astype(BF)
        s_ref[:, j:j + n] = hot[:, :n]
    for b in range(NB):
        sub = lax.broadcasted_iota(jnp.int32, (OWN, NI), 0) + b * OWN
        st_ref[b * OWN:(b + 1) * OWN, :] = jnp.where(sub == pos, 1.0, 0.0).astype(BF)

    def by_rows(rows, fn):
        def step(i, carry):
            fn(pl.ds(pl.multiple_of(i * OWN, OWN), OWN))
            return carry
        lax.fori_loop(0, rows // OWN, step, 0)

    def times_s(src, dst):
        def one(at):
            dst[at, :] = mm(src[at, :], s_ref[...]).astype(BF)
        by_rows(NI, one)

    def recv(dst, sem):
        return remote(dst, dst, sem, sem, (r, c)).wait_recv

    def rows_of(b):
        return slice(b * OWN, (b + 1) * OWN)

    def scatter(value, send, land, ss, rs, s):
        tv_ref[...] = value.astype(BF)
        for b in nbrs:
            send[s, b] = mm(st_ref[rows_of(b), :], tv_ref[...]).astype(BF)
            desc = remote(send.at[s, b], land.at[s, mirror(b)], ss.at[s, b],
                          rs.at[s, mirror(b)], target[b])
            guarded(oks[b], desc.start)
            finals.append((oks[b], desc.wait_send))
        tl_ref[...] = (value - tv_ref[...].astype(F32)).astype(BF)
        mine = st_ref[rows_of(own), :]
        return mm(mine, tv_ref[...]) + mm(mine, tl_ref[...])

    cpos = (cids_ref[...].astype(F32) - (rf - 1.0) * NR).astype(jnp.int32)
    pt = jnp.where(
        lax.broadcasted_iota(jnp.int32, (n_c, cpos.shape[1]), 0) == cpos, 1.0, 0.0
    ).astype(BF)
    pb = mm(pt, basis_ref[...]).astype(BF)
    for b in nbrs + [own]:
        block = lax.dot_general(pb, st_ref[rows_of(b), :], NT, preferred_element_type=F32)
        if b == own:
            pbr[own] = block.astype(BF)
        else:
            pbs[b] = block.astype(BF)
            desc = remote(pbs.at[b], pbr.at[mirror(b)], s_b.at[b], r_b.at[mirror(b)], target[b])
            guarded(oks[b], desc.start)
            finals.append((oks[b], desc.wait_send))

    copy_k.wait()
    times_s(kv, t_ref)

    for s in range(ITERS):
        for b in nbrs:
            guarded(oks[b], recv(xw.at[s, b], r_x.at[s, b]))
        terms = loads_ref[...].astype(F32) - mm(t_ref[...], xw[s].reshape(WN, COLS))
        r_out[...] = scatter(terms, psend, precv, s_p, r_p, s)
        if s == 0:
            flat = jnp.concatenate(
                [panel_ref[a * B + b] for b in range(B) for a in range(A)], axis=0)
            pan_ref[...] = jnp.transpose(flat).astype(BF)
            cw[c, 2] = pan_ref[...]
            for (e, j), dev in far.items():
                desc = remote(pan_ref, cw.at[c, 4 - e], s_w.at[e, j], r_w.at[4 - e, j], dev)
                guarded(row_ok5(e), desc.start)
                finals.append((row_ok5(e), desc.wait_send))
            for b in nbrs:
                guarded(oks[b], recv(idw.at[b], r_id.at[b]))
            mine = lax.broadcasted_iota(jnp.int32, (OWN, 128), 0) + (r * C + c) * OWN
            acc = jnp.zeros((OWN, 128), F32)
            for b in range(NB):
                for j in range(0, NI, 128):
                    acc = acc + jnp.where(idw[b, :, j:j + 128] == mine, 1.0, 0.0)
            count = jnp.sum(acc, axis=1, keepdims=True)
            inv_ref[...] = jnp.broadcast_to(1.0 / jnp.maximum(count, 1.0), (OWN, COLS))
            copy_m.wait()
            times_s(mv, t2_ref)
            for b in nbrs:
                guarded(oks[b], recv(pbr.at[b], r_b.at[b]))
            for b in range(NB):
                qt[b] = jnp.transpose(pbr[b].astype(F32)).astype(BF)
        for b in nbrs:
            guarded(oks[b], recv(precv.at[s, b], r_p.at[s, b]))

            def add(b=b):
                r_out[...] = r_out[...] + precv[s, b].astype(F32)
            guarded(oks[b], add)
        z = (inv_ref[...] * r_out[...]).astype(BF)
        rw[s, own] = z
        bands = [None] * 5
        for b in range(NB):
            part = mm(pbr[b], z).reshape(3, C, NCD, COLS)
            for dd in range(3):
                e = b // W + dd
                bands[e] = part[dd] if bands[e] is None else bands[e] + part[dd]
        for e in range(5):
            csend[s, e * C:(e + 1) * C] = bands[e]
        for (e, j), dev in far.items():
            desc = remote(csend.at[s, e * C + dev[1]], crecv.at[s, 4 - e, j],
                          s_c.at[s, e, j], r_c.at[s, 4 - e, j], dev)
            guarded(row_ok5(e), desc.start)
            finals.append((row_ok5(e), desc.wait_send))
        send_all(lambda b: remote(
            rw.at[s, own], rw.at[s, mirror(b)], s_r.at[s, b], r_r.at[s, mirror(b)], target[b]))
        crecv[s, 2, 0] = csend[s, 2 * C + c]
        for e, j in far:
            guarded(row_ok5(e), recv(crecv.at[s, e, j], r_c.at[s, e, j]))

            def add_c(e=e, j=j):
                crecv[s, 2, 0] = crecv[s, 2, 0] + crecv[s, e, j]
            guarded(row_ok5(e), add_c)
        g_ref[s, c, rb, ra] = crecv[s, 2, 0].astype(BF)
        for i in range(1, A):
            at = g_ref.at[s, c, rb, ra]
            desc = remote(at, at, s_g1.at[s, i], r_g1.at[s, i], g1[i])
            desc.start()
            finals.append((None, desc.wait_send))
        for b in nbrs:
            guarded(oks[b], recv(rw.at[s, b], r_r.at[s, b]))
        acc_ref[...] = scatter(
            mm(t2_ref[...], rw[s].reshape(WN, COLS)), usend, urecv, s_u, r_u, s)
        for i in range(1, A):
            recv(g_ref.at[s, c, rb, (ra + A - i) % A], r_g1.at[s, i])()
        for (j, i), dev in g2.items():
            if (j, i) == (0, 0):
                continue
            at = g_ref.at[s, c, rb]
            desc = remote(at, at, s_g2.at[s, j, i], r_g2.at[s, j, i], dev)
            desc.start()
            finals.append((None, desc.wait_send))
        for (j, i) in g2:
            if (j, i) == (0, 0):
                continue
            recv(g_ref.at[s, (c + C - j) % C, (rb + B - i) % B], r_g2.at[s, j, i])()
        if s == 0:
            for e, j in far:
                guarded(row_ok5(e), recv(cw.at[(c + C - j) % C, e], r_w.at[e, j]))
        sol = None
        for j in range(C):
            rhs = g_ref[s, j].astype(F32).reshape(R * NCD, COLS).astype(BF)
            term = mm(cw[j].reshape(5 * NR, R * NCD), rhs)
            sol = term if sol is None else sol + term
        sol = sol.astype(BF)
        total = acc_ref[...]
        for b in range(NB):
            d = b // W
            total = total + mm(qt[b], sol[d * NR:(d + 3) * NR])
        acc_ref[...] = total
        for b in nbrs:
            guarded(oks[b], recv(urecv.at[s, b], r_u.at[s, b]))

            def add_u(b=b):
                acc_ref[...] = acc_ref[...] + urecv[s, b].astype(F32)
            guarded(oks[b], add_u)
        x_now = (start_ref if s == 0 else x_out)[...] + inv_ref[...] * acc_ref[...]
        x_out[...] = x_now
        if s + 1 < ITERS:
            xw[s + 1, own] = x_now.astype(BF)
            send_x(s + 1)
    for ok, fn in finals:
        guarded(ok, fn)


def solution(mesh):
    R, C = mesh.shape["row"], mesh.shape["col"]
    B = 4 if R % 4 == 0 else (2 if R % 2 == 0 else 1)
    A = R // B
    W = 2 if C == 2 else 3
    NB = 3 * W

    def body(stiffness, local_inverse, averaging_basis, loads, start, coarse_inverse, sizes,
             dof_ids, coarse_ids):
        OWN, COLS = start.shape
        NI = dof_ids.shape[1]
        NCD, NR = coarse_inverse.shape[2:]
        WN = NB * OWN
        panel = coarse_inverse.reshape(R, NCD, NR)
        V = pltpu.VMEM
        D = pltpu.SemaphoreType.DMA
        S = ITERS
        vm = pl.BlockSpec(memory_space=pltpu.VMEM)
        hb = pl.BlockSpec(memory_space=pl.ANY)
        sm = pl.BlockSpec(memory_space=pltpu.SMEM)
        n_c = 3 * NR
        return pl.pallas_call(
            functools.partial(kernel, R, C, B),
            out_shape=(jax.ShapeDtypeStruct((OWN, COLS), F32),) * 2,
            in_specs=[hb, hb, vm, vm, vm, vm, sm, vm, vm],
            out_specs=(vm, vm),
            scratch_shapes=[
                V((NI, NI), BF), V((NI, NI), BF), V((NI, WN), BF), V((WN, NI), BF),
                V((NI, WN), BF), V((NI, WN), BF), V((NI, COLS), BF), V((NI, COLS), BF),
                V((NB, n_c, OWN), BF), V((NB, n_c, OWN), BF), V((NB, OWN, n_c), BF),
                V((NB, 1, NI), jnp.int32), V((S, NB, OWN, COLS), BF), V((S, NB, OWN, COLS), BF),
                V((S, NB, OWN, COLS), BF), V((S, NB, OWN, COLS), BF),
                V((S, NB, OWN, COLS), BF), V((S, NB, OWN, COLS), BF),
                V((S, 5 * C, NCD, COLS), F32), V((S, 5, C, NCD, COLS), F32),
                V((C, 5, NR, R * NCD), BF), V((NR, R * NCD), BF),
                V((S, C, B, A, NCD, COLS), BF),
                V((OWN, COLS), F32), V((OWN, COLS), F32),
                D((2,)), D((NB,)), D((NB,)), D((S, NB)), D((S, NB)), D((S, NB)), D((S, NB)),
                D((S, NB)), D((S, NB)), D((S, NB)), D((S, NB)), D((NB,)), D((NB,)),
                D((S, 5, C)), D((S, 5, C)), D((5, C)), D((5, C)),
                D((S, A)), D((S, A)), D((S, C, B)), D((S, C, B)),
            ],
            compiler_params=pltpu.CompilerParams(
                collective_id=0, has_side_effects=True, vmem_limit_bytes=62 << 20
            ),
        )(stiffness[0], local_inverse[0], jnp.swapaxes(averaging_basis[0], 0, 1), loads[0], start, panel, sizes,
          dof_ids, coarse_ids)

    in_specs = (
        P(("row", "col"), None, None),
        P(("row", "col"), None, None),
        P(("row", "col"), None, None),
        P(("row", "col"), None, None),
        P(("row", "col"), None),
        P(None, "col", None, "row"),
        P(("row", "col")),
        P(("row", "col"), None),
        P(("row", "col"), None),
    )
    out_specs = (P(("row", "col"), None), P(("row", "col"), None))
    return jax.shard_map(body, mesh=mesh, in_specs=in_specs, out_specs=out_specs, check_vma=False)
```

time: 83.1 us -> 70.6 us (0.85); the launches traced: 82.6 us -> 69.2 us
  Pallas kernels: 74.9 us -> 64.8 us
  local copies, waits for them, and re-layouts: 5.5 us -> 3.08 us
  other arithmetic: 0.94 us -> 0 us
    pallas_call x1, Pallas kernels: 74.9 us -> 64.8 us  [body(): pl.pallas_call(functools.partial(kernel, R, C, B), out_shape=(jax.ShapeDt...]
    unnamed x3 -> x2, local copies, waits for them, and re-layouts: 4.78 us -> 3.08 us
    convert_element_type x1 -> x0, other arithmetic: 0.94 us -> none  [body(): panel = panel.reshape(NR, R * NCD).astype(BF)]
where the time goes in v2:
time: 70.6 us; the launch traced here: 69.2 us
  Pallas kernels  64.8 us (92%)
  local copies, waits for them, and re-layouts  3.08 us (4%)
  between operations  1.29 us (2%)
    pallas_call x1, Pallas kernels, body(): pl.pallas_call(functools.partial(kernel, R, C, B), out_shape=(jax.ShapeDt...  64.8 us
    unnamed x2, local copies, waits for them, and re-layouts  3.08 us

profile of v2, /device:TPU:0, one launch (start us, length us, event | category | flops | bytes accessed | tf_op | source)
XLA Modules:
  0.0 69.2 jit_solution(7134562001528481020)
XLA Ops:
  1.3 64.8 %shard_map.104 = (f32[192,128]{1,0:T(8,128)}, f32[192,128]{1,0:T(8,128)}) custom-call(bf16[768,768]{1,0:T(8,128)(2,1)} %bitcast.7, bf16[768,768]{1,0:T(8,128)(2,1)} %bitcast.8, bf16[64,768]{1,0:T(8,128)(2,1)} %bitcast.11, bf16[768,128]{1,0:T(8,128)(2,1)} %bitcast.9, f32[192,128]{1,0:T(8,128)} %start_ref.1, f32[16,24,48]{2,1,0:T(8,128)} %bitcast.10, ...), custom_call_target="tpu_custom_call" | custom-call | tf_op jit(solution)/shard_map/pallas_call | solution.py:357
  66.1 1.5 %copy.14 = f32[192,128]{1,0:T(8,128)} copy(f32[192,128]{1,0:T(8,128)} %get-tuple-element.4) | data formatting | bytes 196608
  67.6 1.5 %copy.15 = f32[192,128]{1,0:T(8,128)} copy(f32[192,128]{1,0:T(8,128)} %get-tuple-element.5) | data formatting | bytes 196608

commit v3 on v2

--- a/solution.py
+++ b/solution.py
@@ -22,7 +22,7 @@
     R, C, B,
     k_hbm, m_hbm, basis_ref, loads_ref, start_ref, panel_ref, sizes_ref, ids_ref, cids_ref,
     x_out, r_out,
-    kv, mv, s_ref, st_ref, t_ref, t2_ref, tv_ref, tl_ref, pbs, pbr, qt,
+    kv, mv, s_ref, st_ref, t_ref, t2_ref, tv_ref, tl_ref, pbs, pbl, pbr, qt,
     idw, xw, rw, psend, precv, usend, urecv, csend, crecv, cw, pan_ref, g_ref, inv_ref, acc_ref,
     ld_sem, s_id, r_id, s_x, r_x, s_r, r_r, s_p, r_p, s_u, r_u, s_b, r_b, s_c, r_c, s_w, r_w,
     s_g1, r_g1, s_g2, r_g2,
@@ -73,7 +73,7 @@
         d, k = b // W, b % W
         return (2 - d) * W + (k if W == 2 else 2 - k)
 
-    nbrs = [b for b in range(NB) if b != own]
+    nbrs = sorted((b for b in range(NB) if b != own), key=lambda b: (b % W == own_k, b // W == 1))
     oks = {b: both(row_ok(b // W), col_ok(b % W)) for b in nbrs}
     target = {b: (r + (b // W - 1), col_of(b % W)) for b in nbrs}
 
@@ -124,7 +124,9 @@
 
     ids_i = ids_ref[...]
     live = lax.broadcasted_iota(jnp.int32, (1, NI), 1) < sizes_ref[0]
-    idw[own] = jnp.where(live, ids_i, -1)
+    idw[own, :, :NI] = jnp.where(live, ids_i, -1)
+    NP = cids_ref.shape[1]
+    idw[own, :, NI:NI + NP] = cids_ref[...]
     ids_f = ids_i.astype(F32)
     owner = floor_div(ids_f, OWN)
     orow = floor_div(owner, C)
@@ -138,11 +140,11 @@
 
     for b in nbrs:
         def fill(b=b):
-            idw[b] = jnp.full((1, NI), -1, jnp.int32)
+            idw[b] = jnp.full(idw.shape[1:], -1, jnp.int32)
             for s in range(ITERS):
                 xw[s, b] = jnp.zeros((OWN, COLS), BF)
                 rw[s, b] = jnp.zeros((OWN, COLS), BF)
-            pbr[b] = jnp.zeros((n_c, OWN), BF)
+            pbl[b] = jnp.zeros((NP, OWN), BF)
         unless(oks[b], fill)
     for e in (0, 1, 3, 4):
         def fill_c(e=e):
@@ -150,6 +152,11 @@
                 cw[j, e] = jnp.zeros(cw.shape[2:], BF)
         unless(row_ok5(e), fill_c)
 
+    flat = jnp.concatenate(
+        [panel_ref[a * B + b] for b in range(B) for a in range(A)], axis=0)
+    pan_ref[...] = jnp.transpose(flat).astype(BF)
+    cw[c, 2] = pan_ref[...]
+
     amount = (A - 1) + (C * B - 1)
     for e, j in far:
         ok = row_ok5(e)
@@ -163,6 +170,11 @@
     send_x(0)
     send_all(lambda b: remote(
         idw.at[own], idw.at[mirror(b)], s_id.at[b], r_id.at[mirror(b)], target[b]))
+
+    for (e, j), dev in far.items():
+        desc = remote(pan_ref, cw.at[c, 4 - e], s_w.at[e, j], r_w.at[4 - e, j], dev)
+        guarded(row_ok5(e), desc.start)
+        finals.append((row_ok5(e), desc.wait_send))
 
     pos_col = jnp.transpose(jnp.broadcast_to(pos, (128, NI)))
     WN = NB * OWN
@@ -201,21 +213,19 @@
             guarded(oks[b], desc.start)
             finals.append((oks[b], desc.wait_send))
         tl_ref[...] = (value - tv_ref[...].astype(F32)).astype(BF)
+
+    def own_part():
         mine = st_ref[rows_of(own), :]
         return mm(mine, tv_ref[...]) + mm(mine, tl_ref[...])
 
-    cpos = (cids_ref[...].astype(F32) - (rf - 1.0) * NR).astype(jnp.int32)
-    pt = jnp.where(
-        lax.broadcasted_iota(jnp.int32, (n_c, cpos.shape[1]), 0) == cpos, 1.0, 0.0
-    ).astype(BF)
-    pb = mm(pt, basis_ref[...]).astype(BF)
     for b in nbrs + [own]:
-        block = lax.dot_general(pb, st_ref[rows_of(b), :], NT, preferred_element_type=F32)
+        block = lax.dot_general(
+            basis_ref[...], st_ref[rows_of(b), :], NT, preferred_element_type=F32).astype(BF)
         if b == own:
-            pbr[own] = block.astype(BF)
+            pbl[own] = block
         else:
-            pbs[b] = block.astype(BF)
-            desc = remote(pbs.at[b], pbr.at[mirror(b)], s_b.at[b], r_b.at[mirror(b)], target[b])
+            pbs[b] = block
+            desc = remote(pbs.at[b], pbl.at[mirror(b)], s_b.at[b], r_b.at[mirror(b)], target[b])
             guarded(oks[b], desc.start)
             finals.append((oks[b], desc.wait_send))
 
@@ -226,16 +236,9 @@
         for b in nbrs:
             guarded(oks[b], recv(xw.at[s, b], r_x.at[s, b]))
         terms = loads_ref[...].astype(F32) - mm(t_ref[...], xw[s].reshape(WN, COLS))
-        r_out[...] = scatter(terms, psend, precv, s_p, r_p, s)
+        scatter(terms, psend, precv, s_p, r_p, s)
+        r_out[...] = own_part()
         if s == 0:
-            flat = jnp.concatenate(
-                [panel_ref[a * B + b] for b in range(B) for a in range(A)], axis=0)
-            pan_ref[...] = jnp.transpose(flat).astype(BF)
-            cw[c, 2] = pan_ref[...]
-            for (e, j), dev in far.items():
-                desc = remote(pan_ref, cw.at[c, 4 - e], s_w.at[e, j], r_w.at[4 - e, j], dev)
-                guarded(row_ok5(e), desc.start)
-                finals.append((row_ok5(e), desc.wait_send))
             for b in nbrs:
                 guarded(oks[b], recv(idw.at[b], r_id.at[b]))
             mine = lax.broadcasted_iota(jnp.int32, (OWN, 128), 0) + (r * C + c) * OWN
@@ -248,9 +251,15 @@
             copy_m.wait()
             times_s(mv, t2_ref)
             for b in nbrs:
-                guarded(oks[b], recv(pbr.at[b], r_b.at[b]))
+                guarded(oks[b], recv(pbl.at[b], r_b.at[b]))
             for b in range(NB):
-                qt[b] = jnp.transpose(pbr[b].astype(F32)).astype(BF)
+                first = (rf + float(b // W - 2)) * NR
+                cpos = (idw[b, :, NI:NI + NP].astype(F32) - first).astype(jnp.int32)
+                pt = jnp.where(
+                    lax.broadcasted_iota(jnp.int32, (n_c, NP), 0) == cpos, 1.0, 0.0).astype(BF)
+                block = mm(pt, pbl[b])
+                pbr[b] = block.astype(BF)
+                qt[b] = jnp.transpose(block).astype(BF)
         for b in nbrs:
             guarded(oks[b], recv(precv.at[s, b], r_p.at[s, b]))
 
@@ -289,8 +298,7 @@
             finals.append((None, desc.wait_send))
         for b in nbrs:
             guarded(oks[b], recv(rw.at[s, b], r_r.at[s, b]))
-        acc_ref[...] = scatter(
-            mm(t2_ref[...], rw[s].reshape(WN, COLS)), usend, urecv, s_u, r_u, s)
+        scatter(mm(t2_ref[...], rw[s].reshape(WN, COLS)), usend, urecv, s_u, r_u, s)
         for i in range(1, A):
             recv(g_ref.at[s, c, rb, (ra + A - i) % A], r_g1.at[s, i])()
         for (j, i), dev in g2.items():
@@ -300,6 +308,13 @@
             desc = remote(at, at, s_g2.at[s, j, i], r_g2.at[s, j, i], dev)
             desc.start()
             finals.append((None, desc.wait_send))
+        acc_ref[...] = own_part()
+        for b in nbrs:
+            guarded(oks[b], recv(urecv.at[s, b], r_u.at[s, b]))
+
+            def add_u(b=b):
+                acc_ref[...] = acc_ref[...] + urecv[s, b].astype(F32)
+            guarded(oks[b], add_u)
         for (j, i) in g2:
             if (j, i) == (0, 0):
                 continue
@@ -317,20 +332,18 @@
         for b in range(NB):
             d = b // W
             total = total + mm(qt[b], sol[d * NR:(d + 3) * NR])
-        acc_ref[...] = total
-        for b in nbrs:
-            guarded(oks[b], recv(urecv.at[s, b], r_u.at[s, b]))
-
-            def add_u(b=b):
-                acc_ref[...] = acc_ref[...] + urecv[s, b].astype(F32)
-            guarded(oks[b], add_u)
-        x_now = (start_ref if s == 0 else x_out)[...] + inv_ref[...] * acc_ref[...]
+        x_now = (start_ref if s == 0 else x_out)[...] + inv_ref[...] * total
         x_out[...] = x_now
         if s + 1 < ITERS:
             xw[s + 1, own] = x_now.astype(BF)
             send_x(s + 1)
     for ok, fn in finals:
         guarded(ok, fn)
+
+
+def hand_over(x_in, r_in, x_out, r_out):
+    x_out[...] = x_in[...]
+    r_out[...] = r_in[...]
 
 
 def solution(mesh):
@@ -354,7 +367,8 @@
         hb = pl.BlockSpec(memory_space=pl.ANY)
         sm = pl.BlockSpec(memory_space=pltpu.SMEM)
         n_c = 3 * NR
-        return pl.pallas_call(
+        NP = coarse_ids.shape[1]
+        pair = pl.pallas_call(
             functools.partial(kernel, R, C, B),
             out_shape=(jax.ShapeDtypeStruct((OWN, COLS), F32),) * 2,
             in_specs=[hb, hb, vm, vm, vm, vm, sm, vm, vm],
@@ -362,8 +376,9 @@
             scratch_shapes=[
                 V((NI, NI), BF), V((NI, NI), BF), V((NI, WN), BF), V((WN, NI), BF),
                 V((NI, WN), BF), V((NI, WN), BF), V((NI, COLS), BF), V((NI, COLS), BF),
-                V((NB, n_c, OWN), BF), V((NB, n_c, OWN), BF), V((NB, OWN, n_c), BF),
-                V((NB, 1, NI), jnp.int32), V((S, NB, OWN, COLS), BF), V((S, NB, OWN, COLS), BF),
+                V((NB, NP, OWN), BF), V((NB, NP, OWN), BF),
+                V((NB, n_c, OWN), BF), V((NB, OWN, n_c), BF),
+                V((NB, 1, NI + 128 * pl.cdiv(NP, 128)), jnp.int32), V((S, NB, OWN, COLS), BF), V((S, NB, OWN, COLS), BF),
                 V((S, NB, OWN, COLS), BF), V((S, NB, OWN, COLS), BF),
                 V((S, NB, OWN, COLS), BF), V((S, NB, OWN, COLS), BF),
                 V((S, 5 * C, NCD, COLS), F32), V((S, 5, C, NCD, COLS), F32),
@@ -380,6 +395,12 @@
             ),
         )(stiffness[0], local_inverse[0], jnp.swapaxes(averaging_basis[0], 0, 1), loads[0], start, panel, sizes,
           dof_ids, coarse_ids)
+        return pl.pallas_call(
+            hand_over,
+            out_shape=(jax.ShapeDtypeStruct((OWN, COLS), F32),) * 2,
+            in_specs=[vm, vm],
+            out_specs=(vm, vm),
+        )(*pair)
 
     in_specs = (
         P(("row", "col"), None, None),

time: 70.6 us -> 67.2 us (0.952); the launches traced: 69.2 us -> 67.1 us
  local copies, waits for them, and re-layouts: 3.08 us -> 0 us
  Pallas kernels: 64.8 us -> 65.8 us
    unnamed x2 -> x0, local copies, waits for them, and re-layouts: 3.08 us -> none
    pallas_call x0 -> x1, Pallas kernels: none -> 1.62 us  [body(): pl.pallas_call(hand_over, out_shape=(jax.ShapeDtypeStruct((OWN, COLS), F3...]
where the time goes in v3:
time: 67.2 us; the launch traced here: 67.1 us
  Pallas kernels  65.8 us (98%)
  between operations  1.29 us (2%)
    pallas_call x1, Pallas kernels, body(): pl.pallas_call(functools.partial(kernel, R, C, B), out_shape=(jax.ShapeDt...  64.1 us
    pallas_call x1, Pallas kernels, body(): pl.pallas_call(hand_over, out_shape=(jax.ShapeDtypeStruct((OWN, COLS), F3...  1.62 us

profile of v3, /device:TPU:0, one launch (start us, length us, event | category | flops | bytes accessed | tf_op | source)
XLA Modules:
  0.0 67.1 jit_solution(7946655095624788103)
XLA Ops:
  1.3 64.1 %shard_map.104 = (f32[192,128]{1,0:T(8,128)}, f32[192,128]{1,0:T(8,128)}) custom-call(bf16[768,768]{1,0:T(8,128)(2,1)} %bitcast.7, bf16[768,768]{1,0:T(8,128)(2,1)} %bitcast.8, bf16[64,768]{1,0:T(8,128)(2,1)} %bitcast.11, bf16[768,128]{1,0:T(8,128)(2,1)} %bitcast.9, f32[192,128]{1,0:T(8,128)} %start_ref.1, f32[16,24,48]{2,1,0:T(8,128)} %bitcast.10, ...), custom_call_target="tpu_custom_call" | custom-call | tf_op jit(solution)/shard_map/pallas_call | solution.py:371
  65.4 1.6 %shard_map.105 = (f32[192,128]{1,0:T(8,128)}, f32[192,128]{1,0:T(8,128)}) custom-call(f32[192,128]{1,0:T(8,128)} %get-tuple-element.4.x_in, f32[192,128]{1,0:T(8,128)} %get-tuple-element.5.r_in), custom_call_target="tpu_custom_call" | custom-call | tf_op jit(solution)/shard_map/pallas_call | solution.py:398
